TPU v7x, 256 devices: a whole 4x4x8 slice. The times are simulated.
256 devices in a mesh: space: 64 (over y_hi, z, x), lag: 4 (over y_lo, core).
Axes of the slice: x: 4, y: 4 (y_hi: 2, y_lo: 2; y = y_hi * 2 + y_lo), z: 8, core: 2. Of those that a mesh axis runs over, the one named last changes fastest.
Arguments:
- prior: bfloat16 [8, 4, 64, 8192], P('lag', None, None, 'space'), may hold values from -6 to 6
- obs_value: float32 [65536], P('space'), may hold values from -6 to 6
- obs_weight: float32 [65536], P('space'), may hold values from 0.5 to 4
- obs_coef: float32 [4, 65536], P(None, 'space'), may hold values from 0.1 to 1
- obs_column: int32 [65536], P('space'), may hold values from 0 to 127
- obs_count: int32 [64], P('space'), may hold values from 512 to 1024
- halo_lists: int32 [2, 32768], P(None, 'space'), may hold values from 0 to 1023
- neighbours: int32 [64, 8192], P(None, 'space'), may hold values from 0 to 2047
- localization: float32 [64, 8192], P(None, 'space'), may hold values from 0.05 to 1
Outputs:
- analysis: bfloat16 [8, 4, 64, 8192], P('lag', None, None, 'space')
Inputs may be any that keep to these rules, and one draw needn't show every extreme that they name: `obs_column`: each observation's column within its own tile. `obs_count`: slots at or beyond a tile's count hold no observation. `halo_lists`: slot numbers within the sending tile. `neighbours`: positions in the extended list of the column's tile.
All inputs are finite; a program needn't handle non-finite values.
Results may differ from a plain program's by a relative error of at most 0.0062.
Values may be sent and summed in bfloat16 or wider, within the bound.
No kernel may reach another device: no remote copies, remote signals or barrier semaphores. Data moves between devices by JAX's collectives and lax.ppermute only.
A program may use at most 64 MiB of HBM per device.

v0:
```python
import jax
import jax.numpy as jnp
from jax import lax
from jax.sharding import PartitionSpec as P

NSI = 2


def broadcast(value, axis, root):
    return lax.dynamic_index_in_dim(lax.all_gather(value, axis), root, 0, keepdims=False)


def from_behind(value, axis, by):
    length = lax.axis_size(axis)
    pairs = [(i, i + by) for i in range(length) if 0 <= i + by < length]
    return lax.ppermute(value, axis, pairs)


def copy_for_each(value, axis):
    copies = jnp.broadcast_to(value, (lax.axis_size(axis), *value.shape))
    return lax.all_to_all(copies, axis, split_axis=0, concat_axis=0, tiled=True)


def laid_out(parts, dim):
    lengths = list(parts.shape[1:])
    lengths[dim] *= parts.shape[0]
    return jnp.moveaxis(parts, 0, dim).reshape(lengths)


def gathered_copies(value, axis, dim):
    parts = copy_for_each(value, axis)
    return laid_out(parts, dim)


def matmul(left, right):
    return jnp.einsum("ikc,kjc->ijc", left, right, precision=lax.Precision.HIGHEST)


def observe(newest, coef, column, value, weight, count):
    picked = jnp.take(newest, column, axis=2).astype(jnp.float32)
    hx = jnp.sum(coef[:, None, :] * picked, axis=0)
    mean_hx = jnp.mean(hx, axis=0)
    valid = (jnp.arange(column.shape[0]) < count).astype(jnp.float32)
    pert = ((hx - mean_hx[None, :]) * valid[None, :]).astype(jnp.bfloat16)
    info = jnp.stack([weight * valid, (value - mean_hx) * valid]).astype(jnp.bfloat16)
    return (pert, info)


def solve(ext_pert, ext_info, table, local_weight):
    members = ext_pert.shape[0]
    gathered = jnp.take(ext_pert, table, axis=1)
    ginfo = jnp.take(ext_info, table, axis=1)
    weighted = (
        gathered.astype(jnp.float32) * (local_weight * ginfo[0].astype(jnp.float32))[None]
    ).astype(jnp.bfloat16)
    gram = jnp.einsum("inc,jnc->ijc", gathered, weighted, preferred_element_type=jnp.float32)
    drive = jnp.einsum("inc,nc->ic", weighted, ginfo[1], preferred_element_type=jnp.float32)
    eye = jnp.eye(members, dtype=jnp.float32)[:, :, None]
    matrix = eye + gram / (members - 1)
    scale = jnp.sqrt(jnp.sum(matrix * matrix, axis=(0, 1)))
    ycur = matrix / scale[None, None, :]
    zcur = jnp.broadcast_to(eye, matrix.shape)
    for step in range(NSI):
        smat = 1.5 * eye - 0.5 * matmul(zcur, ycur)
        ycur = matmul(ycur, smat)
        zcur = matmul(smat, zcur)
    inverse = matmul(zcur, zcur) / scale[None, None, :]
    mean_weight = jnp.einsum("ijc,jc->ic", inverse, drive, precision=lax.Precision.HIGHEST) / (
        members - 1
    )
    root = zcur / jnp.sqrt(scale)[None, None, :]
    return (root + mean_weight[:, None, :]).astype(jnp.bfloat16)


def body(
    prior,
    obs_value,
    obs_weight,
    obs_coef,
    obs_column,
    obs_count,
    halo_lists,
    neighbours,
    localization,
):
    lags = lax.axis_size("lag")
    newest = broadcast(prior[-1], "lag", lags - 1)
    pert, info = observe(newest, obs_coef, obs_column, obs_value, obs_weight, obs_count[0])
    upward = (jnp.take(pert, halo_lists[0], axis=1), jnp.take(info, halo_lists[0], axis=1))
    downward = (jnp.take(pert, halo_lists[1], axis=1), jnp.take(info, halo_lists[1], axis=1))
    below_pert, below_info = from_behind((upward[0], upward[1]), "space", 1)
    above_pert, above_info = from_behind((downward[0], downward[1]), "space", -1)
    ext_pert = jnp.concatenate([pert, below_pert, above_pert], axis=1)
    ext_info = jnp.concatenate([info, below_info, above_info], axis=1)
    share = neighbours.shape[1] // lags
    start = lax.axis_index("lag") * share
    table = lax.dynamic_slice_in_dim(neighbours, start, share, 1)
    local_weight = lax.dynamic_slice_in_dim(localization, start, share, 1)
    portion = solve(ext_pert, ext_info, table, local_weight)
    trans = gathered_copies(portion, "lag", 2)
    values = prior.astype(jnp.float32)
    prior_mean = jnp.mean(values, axis=2, keepdims=True)
    prior_pert = (values - prior_mean).astype(jnp.bfloat16)
    mixed = jnp.einsum("lskc,kjc->lsjc", prior_pert, trans, preferred_element_type=jnp.float32)
    return (prior_mean + mixed).astype(jnp.bfloat16)


def solution(mesh):
    return jax.shard_map(
        body,
        mesh=mesh,
        in_specs=(
            P("lag", None, None, "space"),
            P("space"),
            P("space"),
            P(None, "space"),
            P("space"),
            P("space"),
            P(None, "space"),
            P(None, "space"),
            P(None, "space"),
        ),
        out_specs=P("lag", None, None, "space"),
        check_vma=False,
    )
```

profile of v0, /device:TPU:24, one launch (start us, length us, event | category | flops | bytes accessed | tf_op | source)
XLA Modules:
  0.0 109.9 jit_solution(4790467984454114595)
XLA Ops:
  3.7 5.9 %all_gather.3 = bf16[4,4,64,128]{3,2,1,0:T(8,128)(2,1)S(1)} all-gather(bf16[1,4,64,128]{3,2,1,0:T(8,128)(2,1)S(1)} %slice.18), channel_id=1, replica_groups=mesh['space'=64,'lag'=4] {'lag'}, dimensions={0}, use_global_device_ids=true | all-gather | bytes 327680 | tf_op jit(solution)/shard_map/all_gather | solution.py:10
  10.7 3.6 %gather_fusion = bf16[1024,4,64]{2,1,0:T(4,128)(2,1)S(1)} fusion(bf16[4,64,128]{1,0,2:T(4,128)(2,1)S(1)} %bitcast.108, s32[1024]{0:T(1024)S(1)} %fusion.22), kind=kCustom, calls=%fused_computation.4 | custom fusion | bytes 1052672 | tf_op jit(solution)/shard_map/jit(_take)/gather | solution.py:40
  14.3 16.1 %fusion.1 = (f32[64,1024]{0,1:T(8,128)S(1)}, f32[1024]{0:T(1024)S(1)}) fusion(f32[4,1024]{0,1:T(8,128)S(1)} %copy.73, bf16[1024,4,64]{2,1,0:T(4,128)(2,1)S(1)} %gather_fusion, pred[1024]{0:T(1024)(128)(4,1)S(1)} %compare_and_fusion.1), kind=kLoop, calls=%fused_computation.9 | loop fusion | flops 1244160 | bytes 807936 | tf_op jit(solution)/shard_map/reduce_sum | solution.py:41
  30.8 1.3 %gather_fusion.3 = bf16[512,64]{1,0:T(8,128)(2,1)S(1)} fusion(bf16[64,1024]{0,1:T(8,128)(2,1)S(1)} %multiply_convert_fusion.3, s32[1024]{0:T(1024)S(1)} %pad_clamp_fusion.1), kind=kCustom, calls=%fused_computation.clone | custom fusion | bytes 133120 | tf_op jit(solution)/shard_map/jit(_take)/gather | solution.py:89
  32.3 3.4 %collective-permute-start = (bf16[64,512]{0,1:T(8,128)(2,1)S(1)}, bf16[64,512]{0,1:T(8,128)(2,1)S(1)}, u32[]{:S(2)}, u32[]{:S(2)}) collective-permute-start(bf16[64,512]{0,1:T(8,128)(2,1)S(1)} %select_bitcast_fusion.3), channel_id=1, source_target_pairs={{0,4},{4,8},{8,12},{12,16},{16,20},{20,24},{24,28},{28,32},{32,36}... | collective-permute-start | bytes 196616 | tf_op jit(solution)/shard_map/ppermute | solution.py:16
  35.8 1.3 %gather_fusion.4 = bf16[512,64]{1,0:T(8,128)(2,1)S(1)} fusion(bf16[64,1024]{0,1:T(8,128)(2,1)S(1)} %multiply_convert_fusion.3, s32[1024]{0:T(1024)S(1)} %pad_clamp_fusion), kind=kCustom, calls=%fused_computation.2.clone | custom fusion | bytes 133120 | tf_op jit(solution)/shard_map/jit(_take)/gather | solution.py:90
  37.2 9.1 %collective-permute-start.1 = (bf16[64,512]{0,1:T(8,128)(2,1)S(1)}, bf16[64,512]{0,1:T(8,128)(2,1)S(1)}, u32[]{:S(2)}, u32[]{:S(2)}) collective-permute-start(bf16[64,512]{0,1:T(8,128)(2,1)S(1)} %select_bitcast_fusion.2), channel_id=1, source_target_pairs={{4,0},{8,4},{12,8},{16,12},{20,16},{24,20},{28,24},{32,28},{36,32}... | collective-permute-start | bytes 196616 | tf_op jit(solution)/shard_map/ppermute | solution.py:16
  46.7 1.3 %gather_fusion.5 = bf16[512,2]{1,0:T(8,128)(2,1)S(1)} fusion(bf16[2,1024]{0,1:T(8,128)(2,1)S(1)} %copy.78, s32[1024]{0:T(1024)S(1)} %pad_clamp_fusion.1), kind=kCustom, calls=%fused_computation.1.clone | custom fusion | bytes 6144 | tf_op jit(solution)/shard_map/jit(_take)/gather | solution.py:89
  48.2 1.9 %collective-permute-start.2 = (bf16[2,512]{0,1:T(8,128)(2,1)S(1)}, bf16[2,512]{0,1:T(8,128)(2,1)S(1)}, u32[]{:S(2)}, u32[]{:S(2)}) collective-permute-start(bf16[2,512]{0,1:T(8,128)(2,1)S(1)} %select_bitcast_fusion.1), channel_id=1, source_target_pairs={{0,4},{4,8},{8,12},{12,16},{16,20},{20,24},{24,28},{28,32},{32,36}... | collective-permute-start | bytes 6152 | tf_op jit(solution)/shard_map/ppermute | solution.py:16
  50.1 1.3 %gather_fusion.6 = bf16[512,2]{1,0:T(8,128)(2,1)S(1)} fusion(bf16[2,1024]{0,1:T(8,128)(2,1)S(1)} %copy.78, s32[1024]{0:T(1024)S(1)} %pad_clamp_fusion), kind=kCustom, calls=%fused_computation.3.clone | custom fusion | bytes 6144 | tf_op jit(solution)/shard_map/jit(_take)/gather | solution.py:90
  51.6 9.8 %collective-permute-start.3 = (bf16[2,512]{0,1:T(8,128)(2,1)S(1)}, bf16[2,512]{0,1:T(8,128)(2,1)S(1)}, u32[]{:S(2)}, u32[]{:S(2)}) collective-permute-start(bf16[2,512]{0,1:T(8,128)(2,1)S(1)} %select_bitcast_fusion), channel_id=1, source_target_pairs={{4,0},{8,4},{12,8},{16,12},{20,16},{24,20},{28,24},{32,28},{36,32}... | collective-permute-start | bytes 6152 | tf_op jit(solution)/shard_map/ppermute | solution.py:16
  61.7 2.2 %collective-permute-done.3 = bf16[2,512]{0,1:T(8,128)(2,1)S(1)} collective-permute-done((bf16[2,512]{0,1:T(8,128)(2,1)S(1)}, bf16[2,512]{0,1:T(8,128)(2,1)S(1)}, u32[]{:S(2)}, u32[]{:S(2)}) %collective-permute-start.3) | collective-permute-done | bytes 2080 | tf_op jit(solution)/shard_map/ppermute | solution.py:16
  64.0 6.2 %gather_fusion.2 = bf16[2048,2]{1,0:T(8,128)(2,1)S(1)} fusion(bf16[2,2048]{0,1:T(8,128)(2,1)S(1)} %pad_maximum_fusion.1, s32[2048]{0:T(1024)S(1)} %broadcast_clamp_fusion), kind=kCustom, calls=%fused_computation.6 | custom fusion | bytes 24576 | tf_op jit(solution)/shard_map/jit(_take)/gather | solution.py:52
  71.1 6.2 %gather_fusion.1 = bf16[2048,64]{1,0:T(8,128)(2,1)S(1)} fusion(bf16[64,2048]{0,1:T(8,128)(2,1)S(1)} %pad_maximum_fusion, s32[2048]{0:T(1024)S(1)} %broadcast_clamp_fusion), kind=kCustom, calls=%fused_computation.5 | custom fusion | bytes 532480 | tf_op jit(solution)/shard_map/jit(_take)/gather | solution.py:51
  78.5 1.2 %fusion.6 = f32[64,64,32]{0,1,2:T(8,128)S(1)} fusion(f32[64,64]{0,1:T(8,128)S(1)} %fusion.19, f32[64,64]{0,1:T(8,128)S(1)} %fusion.20, f32[64,64,32]{0,1,2:T(8,128)S(1)} %get-tuple-element.18, f32[32]{0:T(128)S(1)} %get-tuple-element.16), kind=kOutput, calls=%fused_computation.20 | convolution fusion | flops 101056512 | bytes 1081472 | tf_op jit(solution)/shard_map/ikc,kjc->ijc/dot_general | solution.py:36
  79.7 1.2 %convolution_bitcast_fusion.1 = f32[64,64,32]{0,1,2:T(8,128)S(1)} fusion(f32[64,64,32]{0,1,2:T(8,128)S(1)} %fusion.6, f32[64,64,32]{0,1,2:T(8,128)S(1)} %get-tuple-element.18, f32[32]{0:T(128)S(1)} %get-tuple-element.16), kind=kOutput, calls=%fused_computation.16 | convolution fusion | flops 100794368 | bytes 1572992 | tf_op jit(solution)/shard_map/ikc,kjc->ijc/dot_general | solution.py:36
  80.9 1.0 convolution_bitcast_fusion.2
  82.4 1.3 %fusion.4 = f32[64,64,32]{0,1,2:T(8,128)S(1)} fusion(f32[64,64,32]{0,1,2:T(8,128)S(1)} %convolution_bitcast_fusion.1, f32[64,64,32]{0,1,2:T(8,128)S(1)} %convolution_bitcast_fusion.2, f32[64,64]{0,1:T(8,128)S(1)} %fusion.19), kind=kOutput, calls=%fused_computation.15 | convolution fusion | flops 100925440 | bytes 1589248 | tf_op jit(solution)/shard_map/ikc,kjc->ijc/dot_general | solution.py:36
  83.6 1.2 %convolution_bitcast_fusion = f32[64,64,32]{0,1,2:T(8,128)S(1)} fusion(f32[64,64,32]{0,1,2:T(8,128)S(1)} %convolution_bitcast_fusion.2, f32[64,64,32]{0,1,2:T(8,128)S(1)} %fusion.4), kind=kOutput, calls=%fused_computation.12 | convolution fusion | flops 100663296 | bytes 1572864 | tf_op jit(solution)/shard_map/ikc,kjc->ijc/dot_general | solution.py:36
  84.8 1.2 %fusion.2 = f32[64,64,32]{0,1,2:T(8,128)S(1)} fusion(f32[64,64,32]{0,1,2:T(8,128)S(1)} %convolution_bitcast_fusion, f32[32]{0:T(128)S(1)} %get-tuple-element.16), kind=kOutput, calls=%fused_computation.11 | convolution fusion | flops 100794368 | bytes 1048704 | tf_op jit(solution)/shard_map/ikc,kjc->ijc/dot_general | solution.py:36
  88.1 2.7 %reshape.140 = bf16[4,2,65536]{2,1,0:T(2,128)(2,1)} reshape(bf16[4,32,64,64]{3,2,1,0:T(8,128)(2,1)S(1)} %broadcast_bitcast_fusion) | data formatting | bytes 2097152
  90.7 3.5 %all-to-all-start = ((bf16[4,2,65536]{2,1,0:T(2,128)(2,1)}), bf16[4,2,65536]{2,1,0:T(2,128)(2,1)S(1)}, u32[]{:S(2)}, u32[]{:S(2)}) async-start(bf16[4,2,65536]{2,1,0:T(2,128)(2,1)} %reshape.140), calls=%async_computation | async-start | bytes 2097152 | tf_op jit(solution)/shard_map/all_to_all | solution.py:21
  94.5 12.4 %all-to-all-done = bf16[4,2,65536]{2,1,0:T(2,128)(2,1)S(1)} async-done(((bf16[4,2,65536]{2,1,0:T(2,128)(2,1)}), bf16[4,2,65536]{2,1,0:T(2,128)(2,1)S(1)}, u32[]{:S(2)}, u32[]{:S(2)}) %all-to-all-start) | async-done | bytes 1048608 | tf_op jit(solution)/shard_map/all_to_all | solution.py:21
  106.9 1.4 %reshape.141 = bf16[4,32,64,64]{3,2,1,0:T(8,128)(2,1)S(1)} reshape(bf16[4,2,65536]{2,1,0:T(2,128)(2,1)S(1)} %all-to-all-done) | data formatting | bytes 2097152
  (68 shorter events, 11.9 us)
Async XLA Ops:
  3.7 26.7 %copy-start.4 = (f32[1024]{0:T(1024)S(1)}, f32[1024]{0:T(1024)}, u32[]{:S(2)}) copy-start(f32[1024]{0:T(1024)} %param.14) | copy-start | bytes 12292
  14.3 32.1 %copy-start.3 = (f32[1024]{0:T(1024)S(1)}, f32[1024]{0:T(1024)}, u32[]{:S(2)}) copy-start(f32[1024]{0:T(1024)} %param.15) | copy-start | bytes 12292
  30.4 31.0 %copy-start.1 = (s32[64,128]{1,0:T(8,128)S(1)}, s32[64,128]{1,0:T(8,128)}, u32[]{:S(2)}) copy-start(s32[64,128]{1,0:T(8,128)} %param.20) | copy-start | bytes 98308
  32.2 38.6 %copy-start.2 = (f32[64,128]{1,0:T(8,128)S(1)}, f32[64,128]{1,0:T(8,128)}, u32[]{:S(2)}) copy-start(f32[64,128]{1,0:T(8,128)} %param.21) | copy-start | bytes 98308
  32.3 38.7 %collective-permute-start = (bf16[64,512]{0,1:T(8,128)(2,1)S(1)}, bf16[64,512]{0,1:T(8,128)(2,1)S(1)}, u32[]{:S(2)}, u32[]{:S(2)}) collective-permute-start(bf16[64,512]{0,1:T(8,128)(2,1)S(1)} %select_bitcast_fusion.3), channel_id=1, source_target_pairs={{0,4},{4,8},{8,12},{12,16},{16,20},{20,24},{24,28},{28,32},{32,36}... | collective-permute-start | bytes 196616 | tf_op jit(solution)/shard_map/ppermute | solution.py:16
  37.2 33.8 %collective-permute-start.1 = (bf16[64,512]{0,1:T(8,128)(2,1)S(1)}, bf16[64,512]{0,1:T(8,128)(2,1)S(1)}, u32[]{:S(2)}, u32[]{:S(2)}) collective-permute-start(bf16[64,512]{0,1:T(8,128)(2,1)S(1)} %select_bitcast_fusion.2), channel_id=1, source_target_pairs={{4,0},{8,4},{12,8},{16,12},{20,16},{24,20},{28,24},{32,28},{36,32}... | collective-permute-start | bytes 196616 | tf_op jit(solution)/shard_map/ppermute | solution.py:16
  48.2 13.6 %collective-permute-start.2 = (bf16[2,512]{0,1:T(8,128)(2,1)S(1)}, bf16[2,512]{0,1:T(8,128)(2,1)S(1)}, u32[]{:S(2)}, u32[]{:S(2)}) collective-permute-start(bf16[2,512]{0,1:T(8,128)(2,1)S(1)} %select_bitcast_fusion.1), channel_id=1, source_target_pairs={{0,4},{4,8},{8,12},{12,16},{16,20},{20,24},{24,28},{28,32},{32,36}... | collective-permute-start | bytes 6152 | tf_op jit(solution)/shard_map/ppermute | solution.py:16
  51.6 12.3 %collective-permute-start.3 = (bf16[2,512]{0,1:T(8,128)(2,1)S(1)}, bf16[2,512]{0,1:T(8,128)(2,1)S(1)}, u32[]{:S(2)}, u32[]{:S(2)}) collective-permute-start(bf16[2,512]{0,1:T(8,128)(2,1)S(1)} %select_bitcast_fusion), channel_id=1, source_target_pairs={{4,0},{8,4},{12,8},{16,12},{20,16},{24,20},{28,24},{32,28},{36,32}... | collective-permute-start | bytes 6152 | tf_op jit(solution)/shard_map/ppermute | solution.py:16
  88.1 6.2 %copy-start = (bf16[2,4,64,128]{3,2,1,0:T(8,128)(2,1)S(1)}, bf16[2,4,64,128]{3,2,1,0:T(8,128)(2,1)}, u32[]{:S(2)}) copy-start(bf16[2,4,64,128]{3,2,1,0:T(8,128)(2,1)} %param.13) | copy-start | bytes 393220
  90.7 16.2 %all-to-all-start = ((bf16[4,2,65536]{2,1,0:T(2,128)(2,1)}), bf16[4,2,65536]{2,1,0:T(2,128)(2,1)S(1)}, u32[]{:S(2)}, u32[]{:S(2)}) async-start(bf16[4,2,65536]{2,1,0:T(2,128)(2,1)} %reshape.140), calls=%async_computation | async-start | bytes 2097152 | tf_op jit(solution)/shard_map/all_to_all | solution.py:21
where the time goes:
time: 112 us; the launch traced here: 110 us
  local copies, waits for them, and re-layouts  31 us (28%)
  starting transfers between devices  27.8 us (25%)
  other arithmetic  19.9 us (18%)
  waiting for transfers between devices  14.6 us (13%)
  matrix products  9.64 us (9%)
  blocking collectives  5.89 us (5%)
  between operations  1.13 us (1%)
    ppermute x4, starting transfers between devices, from_behind(): return lax.ppermute(value, axis, pairs)  24.3 us
    reduce_sum x1, other arithmetic, observe(): hx = jnp.sum(coef[:, None, :] * picked, axis=0)  16.1 us
    all_to_all x1, waiting for transfers between devices, copy_for_each(): return lax.all_to_all(copies, axis, split_axis=0, concat_axis=0, tiled=True)  12.4 us
    dot_general x6, matrix products, matmul(): jnp.einsum('ikc,kjc->ijc', left, right, precision=lax.Precision.HIGHEST)  7.1 us
    gather x2, local copies, waits for them, and re-layouts, solve(): gathered = jnp.take(ext_pert, table, axis=1)  6.8 us
    gather x2, local copies, waits for them, and re-layouts, solve(): ginfo = jnp.take(ext_info, table, axis=1)  6.68 us
    all_gather x1, blocking collectives, broadcast(): lax.all_gather(value, axis)  5.89 us
    unnamed x15, local copies, waits for them, and re-layouts  5.7 us
  transfers between devices with their start and end apart: 5, of which 2 were waited for; matrix products, arithmetic and copies ran while one was open for 11% of the time, Pallas kernels for 0%

commit v1 on v0

v1 whole, which is shorter than its diff:
```python
import functools

import jax
import jax.numpy as jnp
from jax import lax
from jax.experimental import pallas as pl
from jax.experimental.pallas import tpu as pltpu
from jax.sharding import PartitionSpec as P

K = 64
HALF = 64
ROWS = 80
INTERPRET = False
F32 = jnp.float32
BF16 = jnp.bfloat16


def lanes_of(shape):
    return lax.broadcasted_iota(jnp.int32, shape, len(shape) - 1)


def dot(left, right):
    return jnp.dot(left, right, preferred_element_type=F32)


def observe_kernel(flag, count, newest, coef, column, value, weight, lists, own, first, second):
    slots = column.shape[1]
    spec = newest.shape[0]
    halo = lists.shape[1]
    hot = lax.broadcasted_iota(jnp.int32, (128, slots), 0) == column[...]
    hot = jnp.where(hot, 1.0, 0.0).astype(BF16)
    picked = dot(newest[...].reshape(spec * K, 128), hot)
    hx = coef[0:1, :] * picked[0:K]
    for s in range(1, spec):
        hx = hx + coef[s : s + 1, :] * picked[s * K : (s + 1) * K]
    mean = jnp.sum(hx, axis=0, keepdims=True) * (1.0 / K)
    valid = jnp.where(lanes_of((1, slots)) < count[0], 1.0, 0.0)
    pert = (hx - mean) * valid
    info = jnp.concatenate(
        [weight[...] * valid, (value[...] - mean) * valid, jnp.zeros((ROWS - K - 2, slots), F32)],
        axis=0,
    )
    table = jnp.concatenate([pert, info], axis=0).astype(BF16)
    own[...] = table
    blocks = slots // 128
    stacked = jnp.concatenate([table[:, b * 128 : (b + 1) * 128] for b in range(blocks)], axis=0)
    odd = flag[0] == 1
    for out, mine, other in ((first, 0, 1), (second, 1, 0)):
        index = jnp.where(odd, lists[mine : mine + 1, :], lists[other : other + 1, :])
        low = index & 127
        high = index >> 7
        hot = lax.broadcasted_iota(jnp.int32, (128, halo), 0) == low
        found = dot(stacked, jnp.where(hot, 1.0, 0.0).astype(BF16))
        total = found[0:ROWS]
        for b in range(1, blocks):
            total = jnp.where(high == b, found[b * ROWS : (b + 1) * ROWS], total)
        out[...] = total.astype(BF16)


def packed(square, lower):
    left = lanes_of((HALF, 128)) < HALF
    if lower:
        return jnp.where(left, square[0:HALF], pltpu.roll(square[HALF:], HALF, 1))
    return jnp.where(left, pltpu.roll(square[0:HALF], HALF, 1), square[HALF:])


def block_diagonal(pair, left):
    zero = jnp.zeros_like(pair)
    return jnp.concatenate([jnp.where(left, pair, zero), jnp.where(left, zero, pair)], axis=0)


def solve_kernel(
    flag, index, own, first, second, local, prior, out,
    table_a, table_b, rows, matrix, squares, factors, pd, mixed, shift, means, weights,
):
    lags, spec = prior.shape[0], prior.shape[1]
    slots, halo = own.shape[1], first.shape[1]
    odd = flag[0]
    left = lanes_of((HALF, 128)) < HALF

    def put(source, offset, block):
        piece = source[:, block * 128 : (block + 1) * 128].astype(F32)
        piece = jnp.concatenate([piece, jnp.zeros((128 - ROWS, 128), F32)], axis=0).T
        at = pl.multiple_of(offset + block * 128, 128)
        table_a[pl.ds(at, 128), :] = piece
        table_b[pl.ds(at, 128), :] = pltpu.roll(piece, HALF, 1)

    for b in range(slots // 128):
        put(own, 0, b)
    for b in range(halo // 128):
        put(first, slots + odd * halo, b)
        put(second, slots + (1 - odd) * halo, b)

    twice = jnp.concatenate([local[...], local[...]], axis=0).T
    weights[...] = jnp.where(left, twice[0:HALF], twice[HALF:])

    def rank(pair):
        lag, s = pair // spec, pair % spec
        values = prior[lag, s].astype(F32)
        mean = jnp.sum(values, axis=0, keepdims=True) * (1.0 / K)
        means[pair : pair + 1, :] = mean
        return (values - mean).astype(BF16).astype(F32)

    count = lags * spec
    for pair in range(0, count, 2):
        square = jnp.concatenate([rank(pair), rank(pair + 1)], axis=0).T
        pd[pl.ds(pair, HALF, stride=16), :] = packed(square, True)
        pd[pl.ds(pair + 1, HALF, stride=16), :] = packed(square, False)

    row = lax.broadcasted_iota(jnp.int32, (HALF, 128), 0)
    eye = jnp.where(row == (lanes_of((HALF, 128)) & (HALF - 1)), 1.0, 0.0)
    leftb = lanes_of((HALF, 128)) < HALF
    ones = block_diagonal(jnp.ones((HALF, 128), F32), left).astype(BF16)

    @pl.loop(0, HALF)
    def _(q):
        for n in range(HALF):
            rows[n : n + 1, :] = table_a[pl.ds(index[n, q], 1), :]
            rows[HALF + n : HALF + n + 1, :] = table_b[pl.ds(index[n, q + HALF], 1), :]
        found = rows[...]
        across = found.T
        gathered = jnp.where(left, across[0:HALF], across[HALF:])
        top = left[0:1]
        info0 = jnp.where(top, across[HALF : HALF + 1], across[0:1])
        info1 = jnp.where(top, across[HALF + 1 : HALF + 2], across[1:2])
        scaled = weights[pl.ds(q, 1), :] * info0
        weighted = (gathered * scaled).astype(BF16)
        pull = scaled * info1
        pull_high = pull.astype(BF16).astype(F32)
        extra = jnp.concatenate([pull_high, pull - pull_high, jnp.zeros((14, 128), F32)], axis=0)
        lhs = jnp.concatenate([weighted, extra.astype(BF16)], axis=0)
        zero = jnp.zeros((HALF, 128), F32)
        diagonal = jnp.concatenate(
            [jnp.where(left, found[0:HALF], zero), jnp.where(left, zero, found[HALF:])], axis=0
        ).astype(BF16)
        product = dot(lhs, diagonal)
        full = eye + product[0:HALF] * (1.0 / (K - 1))
        matrix[q] = full
        squares[pl.ds(q, 1), :] = jnp.sum(full * full, axis=0, keepdims=True)
        drive = product[HALF : HALF + 1] + product[HALF + 1 : HALF + 2]
        drive_low = drive - drive.astype(BF16).astype(F32)
        tail = jnp.concatenate([drive, drive_low, jnp.zeros((6, 128), F32)], axis=0)
        pd[pl.ds(pl.multiple_of(q * 16 + 8, 8), 8), :] = tail

    def half_sums(values):
        high = values.astype(BF16)
        low = (values - high.astype(F32)).astype(BF16)
        return dot(high, ones) + dot(low, ones)

    scale = jnp.sqrt(half_sums(squares[...]))
    factors[...] = 1.0 / scale

    @pl.loop(0, HALF)
    def _(q):
        a = matrix[q] * factors[pl.ds(q, 1), :]
        ab = a.astype(BF16)
        b = dot(ab, block_diagonal(ab, leftb))
        c = -0.5625 * a + 0.0625 * b
        z = dot(c.astype(BF16), block_diagonal(b.astype(BF16), leftb))
        z = z + 2.25 * eye - 2.4375 * a + 1.6875 * b
        lhs = pd[pl.ds(pl.multiple_of(q * 16, 16), 16), :].astype(BF16)
        product = dot(lhs, block_diagonal(z.astype(BF16), leftb))
        mix = product[0:8]
        pulled = product[8:9] + product[9:10]
        at = pl.ds(pl.multiple_of(q * 8, 8), 8)
        mixed[at, :] = mix
        shift[at, :] = mix * pulled

    shift[...] = half_sums(shift[...])
    one = factors[...]
    root = jnp.sqrt(one)
    one = one * (1.0 / (K - 1))

    def final(pair):
        at = pl.ds(pair, HALF, stride=8)
        return mixed[at, :] * root + shift[at, :] * one

    for pair in range(0, count, 2):
        square = jnp.concatenate([final(pair), final(pair + 1)], axis=0).T
        for which in range(2):
            lag, s = (pair + which) // spec, (pair + which) % spec
            value = packed(square, which == 0) + means[pair + which : pair + which + 1, :]
            out[lag, s] = value.astype(BF16)


def vmem():
    return pl.BlockSpec(memory_space=pltpu.VMEM)


def smem():
    return pl.BlockSpec(memory_space=pltpu.SMEM)


def observe(flag, count, newest, coef, column, value, weight, lists):
    slots, halo = column.shape[0], lists.shape[1]
    shapes = [(ROWS, slots), (ROWS, halo), (ROWS, halo)]
    return pl.pallas_call(
        observe_kernel,
        out_shape=[jax.ShapeDtypeStruct(s, BF16) for s in shapes],
        in_specs=[smem(), smem()] + [vmem()] * 6,
        out_specs=[vmem()] * 3,
        interpret=INTERPRET,
        name="observe",
    )(flag, count, newest, coef, column[None], value[None], weight[None], lists)


def solve(flag, index, own, first, second, local, prior):
    positions = own.shape[1] + 2 * first.shape[1]
    return pl.pallas_call(
        solve_kernel,
        out_shape=jax.ShapeDtypeStruct(prior.shape, BF16),
        in_specs=[smem(), smem()] + [vmem()] * 5,
        out_specs=vmem(),
        scratch_shapes=[
            pltpu.VMEM((positions, 128), F32),
            pltpu.VMEM((positions, 128), F32),
            pltpu.VMEM((128, 128), F32),
            pltpu.VMEM((HALF, HALF, 128), F32),
            pltpu.VMEM((HALF, 128), F32),
            pltpu.VMEM((HALF, 128), F32),
            pltpu.VMEM((HALF * 16, 128), F32),
            pltpu.VMEM((HALF * 8, 128), F32),
            pltpu.VMEM((HALF * 8, 128), F32),
            pltpu.VMEM((8, 128), F32),
            pltpu.VMEM((HALF, 128), F32),
        ],
        interpret=INTERPRET,
        name="solve",
    )(flag, index, own, first, second, local, prior)


def swaps(length, start):
    pairs = []
    for low in range(start, length - 1, 2):
        pairs += [(low, low + 1), (low + 1, low)]
    return pairs


def body(
    prior,
    obs_value,
    obs_weight,
    obs_coef,
    obs_column,
    obs_count,
    halo_lists,
    neighbours,
    localization,
):
    lags = lax.axis_size("lag")
    tiles = lax.axis_size("space")
    flag = (lax.axis_index("space") % 2)[None].astype(jnp.int32)
    newest = lax.all_gather(prior[-1], "lag")[lags - 1]
    own, first, second = observe(
        flag, obs_count, newest, obs_coef, obs_column, obs_value, obs_weight, halo_lists
    )
    first = lax.ppermute(first, "space", swaps(tiles, 1))
    second = lax.ppermute(second, "space", swaps(tiles, 0))
    return solve(flag, neighbours, own, first, second, localization, prior)


def solution(mesh):
    return jax.shard_map(
        body,
        mesh=mesh,
        in_specs=(
            P("lag", None, None, "space"),
            P("space"),
            P("space"),
            P(None, "space"),
            P("space"),
            P("space"),
            P(None, "space"),
            P(None, "space"),
            P(None, "space"),
        ),
        out_specs=P("lag", None, None, "space"),
        check_vma=False,
    )
```

time: 112 us -> 78.5 us (0.70); the launches traced: 110 us -> 78.2 us
  Pallas kernels: 0 us -> 54.3 us
  local copies, waits for them, and re-layouts: 31 us -> 2.1 us
  other arithmetic: 19.9 us -> 0 us
  starting transfers between devices: 27.8 us -> 10.7 us
  waiting for transfers between devices: 14.6 us -> 4.64 us
  matrix products: 9.64 us -> 0 us
    pallas_call x0 -> x2, Pallas kernels: none -> 54.3 us  [the longest x1 52 us: solve(): pl.pallas_call(solve_kernel, out_shape=jax.ShapeDtypeStruct(prior.shape,...]
    gather x9 -> x0, local copies, waits for them, and re-layouts: 22.4 us -> none  [the longest x2 6.8 us: solve(): gathered = jnp.take(ext_pert, table, axis=1)]
    reduce_sum x2 -> x0, other arithmetic: 16.2 us -> none  [the longest x1 16.1 us: observe(): hx = jnp.sum(coef[:, None, :] * picked, axis=0)]
    ppermute x4 -> x2, starting transfers between devices: 24.3 us -> 10.7 us  [the longest x1 10.6 us: body(): first = lax.ppermute(first, 'space', swaps(tiles, 1))]
    all_to_all x1 -> x0, waiting for transfers between devices: 12.4 us -> none  [copy_for_each(): return lax.all_to_all(copies, axis, split_axis=0, concat_axis=0, tiled=True)]
    dot_general x10 -> x0, matrix products: 9.64 us -> none  [the longest x6 7.1 us: matmul(): jnp.einsum('ikc,kjc->ijc', left, right, precision=lax.Precision.HIGHEST)]
    unnamed x15 -> x4, local copies, waits for them, and re-layouts: 5.7 us -> 0.64 us
    all_to_all x1 -> x0, starting transfers between devices: 3.5 us -> none  [copy_for_each(): return lax.all_to_all(copies, axis, split_axis=0, concat_axis=0, tiled=True)]
  transfers between devices with their start and end apart: 5 -> 2, of which waited for: 2 -> 2; matrix products, arithmetic and copies ran while one was open for 11% -> 0% of each run, Pallas kernels for 0% -> 0%
where the time goes in v1:
time: 78.5 us; the launch traced here: 78.2 us
  Pallas kernels  54.3 us (69%)
  starting transfers between devices  10.7 us (14%)
  blocking collectives  5.76 us (7%)
  waiting for transfers between devices  4.64 us (6%)
  local copies, waits for them, and re-layouts  2.1 us (3%)
    pallas_call x1, Pallas kernels, solve(): pl.pallas_call(solve_kernel, out_shape=jax.ShapeDtypeStruct(prior.shape,...  52 us
    ppermute x1, starting transfers between devices, body(): first = lax.ppermute(first, 'space', swaps(tiles, 1))  10.6 us
    all_gather x1, blocking collectives, body(): newest = lax.all_gather(prior[-1], 'lag')[lags - 1]  5.76 us
    ppermute x1, waiting for transfers between devices, body(): first = lax.ppermute(first, 'space', swaps(tiles, 1))  3.05 us
    pallas_call x1, Pallas kernels, observe(): pl.pallas_call(observe_kernel, out_shape=[jax.ShapeDtypeStruct(s, BF16) f...  2.31 us
    ppermute x1, waiting for transfers between devices, body(): second = lax.ppermute(second, 'space', swaps(tiles, 0))  1.59 us
  transfers between devices with their start and end apart: 2, of which 2 were waited for; matrix products, arithmetic and copies ran while one was open for 0% of the time, Pallas kernels for 0%

profile of v1, /device:TPU:24, one launch (start us, length us, event | category | flops | bytes accessed | tf_op | source)
XLA Modules:
  0.0 78.2 jit_solution(12857737194162990663)
XLA Ops:
  0.7 0.0 slice-start
  0.7 0.8 %slice-done = bf16[1,4,64,128]{3,2,1,0:T(8,128)(2,1)S(1)} async-done(((bf16[2,4,64,128]{3,2,1,0:T(8,128)(2,1)}), bf16[1,4,64,128]{3,2,1,0:T(8,128)(2,1)S(1)}, s32[]{:S(2)}) %slice-start) | async-done | bytes 65560 | tf_op jit(solution)/shard_map/slice | solution.py:253
  1.5 5.8 %all_gather.3 = bf16[4,4,64,128]{3,2,1,0:T(8,128)(2,1)S(1)} all-gather(bf16[1,4,64,128]{3,2,1,0:T(8,128)(2,1)S(1)} %slice-done), channel_id=1, replica_groups=mesh['space'=64,'lag'=4] {'lag'}, dimensions={0}, use_global_device_ids=true | all-gather | bytes 327680 | tf_op jit(solution)/shard_map/all_gather | solution.py:253
  7.3 0.6 slice_bitcast_fusion.newest
  7.9 2.3 %observe.1 = (bf16[80,1024]{1,0:T(8,128)(2,1)}, bf16[80,512]{1,0:T(8,128)(2,1)}, bf16[80,512]{1,0:T(8,128)(2,1)}) custom-call(s32[1]{0:T(128)} %bitcast.flag, s32[1]{0:T(128)S(6)} %copy.10.count, bf16[4,64,128]{2,1,0:T(8,128)(2,1)} %slice_bitcast_fusion.newest, f32[4,1024]{1,0:T(4,128)} %coef.1, s32[1,1024]{1,0:T(1,128)} %bitcast.6, f32[1,1024]{1,0:T(1,128)} %bitcast.7, ...), custom_call_target="tpu_custom_call" | custom-call | tf_op jit(solution)/shard_map/observe/pallas_call | solution.py:197
  10.2 10.6 %collective-permute-start = (bf16[80,512]{1,0:T(8,128)(2,1)}, bf16[80,512]{1,0:T(8,128)(2,1)S(1)}, u32[]{:S(2)}, u32[]{:S(2)}) collective-permute-start(bf16[80,512]{1,0:T(8,128)(2,1)} %get-tuple-element.9), channel_id=1, source_target_pairs={{4,8},{8,4},{12,16},{16,12},{20,24},{24,20},{28,32},{32,28},{36,40... | collective-permute-start | bytes 245768 | tf_op jit(solution)/shard_map/ppermute | solution.py:257
  20.8 0.1 collective-permute-start.1
  20.9 3.0 %collective-permute-done.first = bf16[80,512]{1,0:T(8,128)(2,1)S(1)} collective-permute-done((bf16[80,512]{1,0:T(8,128)(2,1)}, bf16[80,512]{1,0:T(8,128)(2,1)S(1)}, u32[]{:S(2)}, u32[]{:S(2)}) %collective-permute-start) | collective-permute-done | bytes 81952 | tf_op jit(solution)/shard_map/ppermute | solution.py:257
  24.0 0.0 copy-start
  24.0 1.6 %collective-permute-done.1.second = bf16[80,512]{1,0:T(8,128)(2,1)S(1)} collective-permute-done((bf16[80,512]{1,0:T(8,128)(2,1)}, bf16[80,512]{1,0:T(8,128)(2,1)S(1)}, u32[]{:S(2)}, u32[]{:S(2)}) %collective-permute-start.1) | collective-permute-done | bytes 81952 | tf_op jit(solution)/shard_map/ppermute | solution.py:258
  25.6 0.0 copy-start.1
  25.6 0.0 copy-done
  25.6 0.6 copy-done.1
  26.2 52.0 %solve.1 = bf16[2,4,64,128]{3,2,1,0:T(8,128)(2,1)} custom-call(s32[1]{0:T(128)} %bitcast.flag, s32[64,128]{1,0:T(8,128)} %index.1, bf16[80,1024]{1,0:T(8,128)(2,1)} %get-tuple-element.8.own, bf16[80,512]{1,0:T(8,128)(2,1)} %copy-done, bf16[80,512]{1,0:T(8,128)(2,1)} %copy-done.1, f32[64,128]{1,0:T(8,128)} %local.1, bf16[2,4,64,128]{3,2,1,0:T(8,128)(2,1)} %prior.1), custom_call_target="tpu_custom_call" | custom-call | tf_op jit(solution)/shard_map/solve/pallas_call | solution.py:209
Async XLA Ops:
  0.7 0.8 %slice-start = ((bf16[2,4,64,128]{3,2,1,0:T(8,128)(2,1)}), bf16[1,4,64,128]{3,2,1,0:T(8,128)(2,1)S(1)}, s32[]{:S(2)}) async-start(bf16[2,4,64,128]{3,2,1,0:T(8,128)(2,1)} %prior.1), calls=%async_computation | async-start | bytes 131072 | tf_op jit(solution)/shard_map/slice | solution.py:253
  10.2 13.8 %collective-permute-start = (bf16[80,512]{1,0:T(8,128)(2,1)}, bf16[80,512]{1,0:T(8,128)(2,1)S(1)}, u32[]{:S(2)}, u32[]{:S(2)}) collective-permute-start(bf16[80,512]{1,0:T(8,128)(2,1)} %get-tuple-element.9), channel_id=1, source_target_pairs={{4,8},{8,4},{12,16},{16,12},{20,24},{24,20},{28,32},{32,28},{36,40... | collective-permute-start | bytes 245768 | tf_op jit(solution)/shard_map/ppermute | solution.py:257
  20.8 4.7 %collective-permute-start.1 = (bf16[80,512]{1,0:T(8,128)(2,1)}, bf16[80,512]{1,0:T(8,128)(2,1)S(1)}, u32[]{:S(2)}, u32[]{:S(2)}) collective-permute-start(bf16[80,512]{1,0:T(8,128)(2,1)} %get-tuple-element.10), channel_id=1, source_target_pairs={{0,4},{4,0},{8,12},{12,8},{16,20},{20,16},{24,28},{28,24},{32,36},... | collective-permute-start | bytes 245768 | tf_op jit(solution)/shard_map/ppermute | solution.py:258
  24.0 1.6 %copy-start = (bf16[80,512]{1,0:T(8,128)(2,1)}, bf16[80,512]{1,0:T(8,128)(2,1)S(1)}, u32[]{:S(2)}) copy-start(bf16[80,512]{1,0:T(8,128)(2,1)S(1)} %collective-permute-done.first) | copy-start | bytes 245764
  25.6 0.6 copy-start.1

commit v2 on v1

--- a/solution.py
+++ b/solution.py
@@ -10,6 +10,8 @@
 K = 64
 HALF = 64
 ROWS = 80
+UA = 16
+UC = 16
 INTERPRET = False
 F32 = jnp.float32
 BF16 = jnp.bfloat16
@@ -112,35 +114,40 @@
     leftb = lanes_of((HALF, 128)) < HALF
     ones = block_diagonal(jnp.ones((HALF, 128), F32), left).astype(BF16)
 
-    @pl.loop(0, HALF)
-    def _(q):
-        for n in range(HALF):
-            rows[n : n + 1, :] = table_a[pl.ds(index[n, q], 1), :]
-            rows[HALF + n : HALF + n + 1, :] = table_b[pl.ds(index[n, q + HALF], 1), :]
-        found = rows[...]
-        across = found.T
-        gathered = jnp.where(left, across[0:HALF], across[HALF:])
+    @pl.loop(0, HALF // UA)
+    def _(step):
+        qs = [step * UA + u for u in range(UA)]
+        for u, q in enumerate(qs):
+            for n in range(HALF):
+                rows[u, n : n + 1, :] = table_a[pl.ds(index[n, q], 1), :]
+                rows[u, HALF + n : HALF + n + 1, :] = table_b[pl.ds(index[n, q + HALF], 1), :]
+        lefts, diagonals = [], []
         top = left[0:1]
-        info0 = jnp.where(top, across[HALF : HALF + 1], across[0:1])
-        info1 = jnp.where(top, across[HALF + 1 : HALF + 2], across[1:2])
-        scaled = weights[pl.ds(q, 1), :] * info0
-        weighted = (gathered * scaled).astype(BF16)
-        pull = scaled * info1
-        pull_high = pull.astype(BF16).astype(F32)
-        extra = jnp.concatenate([pull_high, pull - pull_high, jnp.zeros((14, 128), F32)], axis=0)
-        lhs = jnp.concatenate([weighted, extra.astype(BF16)], axis=0)
         zero = jnp.zeros((HALF, 128), F32)
-        diagonal = jnp.concatenate(
-            [jnp.where(left, found[0:HALF], zero), jnp.where(left, zero, found[HALF:])], axis=0
-        ).astype(BF16)
-        product = dot(lhs, diagonal)
-        full = eye + product[0:HALF] * (1.0 / (K - 1))
-        matrix[q] = full
-        squares[pl.ds(q, 1), :] = jnp.sum(full * full, axis=0, keepdims=True)
-        drive = product[HALF : HALF + 1] + product[HALF + 1 : HALF + 2]
-        drive_low = drive - drive.astype(BF16).astype(F32)
-        tail = jnp.concatenate([drive, drive_low, jnp.zeros((6, 128), F32)], axis=0)
-        pd[pl.ds(pl.multiple_of(q * 16 + 8, 8), 8), :] = tail
+        for u, q in enumerate(qs):
+            found = rows[u]
+            across = found.T
+            gathered = jnp.where(left, across[0:HALF], across[HALF:])
+            info0 = jnp.where(top, across[HALF : HALF + 1], across[0:1])
+            info1 = jnp.where(top, across[HALF + 1 : HALF + 2], across[1:2])
+            scaled = weights[pl.ds(q, 1), :] * info0
+            weighted = (gathered * scaled).astype(BF16)
+            pull = scaled * info1
+            pull_high = pull.astype(BF16).astype(F32)
+            extra = jnp.concatenate([pull_high, pull - pull_high, jnp.zeros((14, 128), F32)], axis=0)
+            lefts.append(jnp.concatenate([weighted, extra.astype(BF16)], axis=0))
+            diagonals.append(jnp.concatenate(
+                [jnp.where(left, found[0:HALF], zero), jnp.where(left, zero, found[HALF:])], axis=0
+            ).astype(BF16))
+        products = [dot(l, d) for l, d in zip(lefts, diagonals)]
+        for q, product in zip(qs, products):
+            full = eye + product[0:HALF] * (1.0 / (K - 1))
+            matrix[q] = full
+            squares[pl.ds(q, 1), :] = jnp.sum(full * full, axis=0, keepdims=True)
+            drive = product[HALF : HALF + 1] + product[HALF + 1 : HALF + 2]
+            drive_low = drive - drive.astype(BF16).astype(F32)
+            tail = jnp.concatenate([drive, drive_low, jnp.zeros((6, 128), F32)], axis=0)
+            pd[pl.ds(pl.multiple_of(q * 16 + 8, 8), 8), :] = tail
 
     def half_sums(values):
         high = values.astype(BF16)
@@ -150,21 +157,26 @@
     scale = jnp.sqrt(half_sums(squares[...]))
     factors[...] = 1.0 / scale
 
-    @pl.loop(0, HALF)
-    def _(q):
-        a = matrix[q] * factors[pl.ds(q, 1), :]
-        ab = a.astype(BF16)
-        b = dot(ab, block_diagonal(ab, leftb))
-        c = -0.5625 * a + 0.0625 * b
-        z = dot(c.astype(BF16), block_diagonal(b.astype(BF16), leftb))
-        z = z + 2.25 * eye - 2.4375 * a + 1.6875 * b
-        lhs = pd[pl.ds(pl.multiple_of(q * 16, 16), 16), :].astype(BF16)
-        product = dot(lhs, block_diagonal(z.astype(BF16), leftb))
-        mix = product[0:8]
-        pulled = product[8:9] + product[9:10]
-        at = pl.ds(pl.multiple_of(q * 8, 8), 8)
-        mixed[at, :] = mix
-        shift[at, :] = mix * pulled
+    @pl.loop(0, HALF // UC)
+    def _(step):
+        qs = [step * UC + u for u in range(UC)]
+        first_powers = [matrix[q] * factors[pl.ds(q, 1), :] for q in qs]
+        halves = [a.astype(BF16) for a in first_powers]
+        second_powers = [dot(a, block_diagonal(a, leftb)) for a in halves]
+        mixes = [(-0.5625 * a + 0.0625 * b).astype(BF16) for a, b in zip(first_powers, second_powers)]
+        zs = [dot(c, block_diagonal(b.astype(BF16), leftb)) for c, b in zip(mixes, second_powers)]
+        zs = [
+            z + 2.25 * eye - 2.4375 * a + 1.6875 * b
+            for z, a, b in zip(zs, first_powers, second_powers)
+        ]
+        sides = [pd[pl.ds(pl.multiple_of(q * 16, 16), 16), :].astype(BF16) for q in qs]
+        products = [dot(p, block_diagonal(z.astype(BF16), leftb)) for p, z in zip(sides, zs)]
+        for q, product in zip(qs, products):
+            mix = product[0:8]
+            pulled = product[8:9] + product[9:10]
+            at = pl.ds(pl.multiple_of(q * 8, 8), 8)
+            mixed[at, :] = mix
+            shift[at, :] = mix * pulled
 
     shift[...] = half_sums(shift[...])
     one = factors[...]
@@ -214,7 +226,7 @@
         scratch_shapes=[
             pltpu.VMEM((positions, 128), F32),
             pltpu.VMEM((positions, 128), F32),
-            pltpu.VMEM((128, 128), F32),
+            pltpu.VMEM((UA, 128, 128), F32),
             pltpu.VMEM((HALF, HALF, 128), F32),
             pltpu.VMEM((HALF, 128), F32),
             pltpu.VMEM((HALF, 128), F32),

time: 78.5 us -> 43 us (0.55)
  Pallas kernels: 54.3 us -> 18.9 us
    pallas_call x1, Pallas kernels: 52 us -> 16.6 us  [solve(): pl.pallas_call(solve_kernel, out_shape=jax.ShapeDtypeStruct(prior.shape,...]
where the time goes in v2:
time: 43 us; the launch traced here: 42.8 us
  Pallas kernels  18.9 us (44%)
  starting transfers between devices  10.7 us (25%)
  blocking collectives  5.76 us (13%)
  waiting for transfers between devices  4.64 us (11%)
  local copies, waits for them, and re-layouts  2.1 us (5%)
  between operations  0.68 us (2%)
    pallas_call x1, Pallas kernels, solve(): pl.pallas_call(solve_kernel, out_shape=jax.ShapeDtypeStruct(prior.shape,...  16.6 us
    ppermute x1, starting transfers between devices, body(): first = lax.ppermute(first, 'space', swaps(tiles, 1))  10.6 us
    all_gather x1, blocking collectives, body(): newest = lax.all_gather(prior[-1], 'lag')[lags - 1]  5.76 us
    ppermute x1, waiting for transfers between devices, body(): first = lax.ppermute(first, 'space', swaps(tiles, 1))  3.05 us
    pallas_call x1, Pallas kernels, observe(): pl.pallas_call(observe_kernel, out_shape=[jax.ShapeDtypeStruct(s, BF16) f...  2.31 us
    ppermute x1, waiting for transfers between devices, body(): second = lax.ppermute(second, 'space', swaps(tiles, 0))  1.59 us
  transfers between devices with their start and end apart: 2, of which 2 were waited for; matrix products, arithmetic and copies ran while one was open for 0% of the time, Pallas kernels for 0%

profile of v2, /device:TPU:24, one launch (start us, length us, event | category | flops | bytes accessed | tf_op | source)
XLA Modules:
  0.0 42.8 jit_solution(15804689081271199697)
XLA Ops:
  0.7 0.0 slice-start
  0.7 0.8 %slice-done = bf16[1,4,64,128]{3,2,1,0:T(8,128)(2,1)S(1)} async-done(((bf16[2,4,64,128]{3,2,1,0:T(8,128)(2,1)}), bf16[1,4,64,128]{3,2,1,0:T(8,128)(2,1)S(1)}, s32[]{:S(2)}) %slice-start) | async-done | bytes 65560 | tf_op jit(solution)/shard_map/slice | solution.py:265
  1.5 5.8 %all_gather.3 = bf16[4,4,64,128]{3,2,1,0:T(8,128)(2,1)S(1)} all-gather(bf16[1,4,64,128]{3,2,1,0:T(8,128)(2,1)S(1)} %slice-done), channel_id=1, replica_groups=mesh['space'=64,'lag'=4] {'lag'}, dimensions={0}, use_global_device_ids=true | all-gather | bytes 327680 | tf_op jit(solution)/shard_map/all_gather | solution.py:265
  7.3 0.6 %slice_bitcast_fusion.newest = bf16[4,64,128]{2,1,0:T(8,128)(2,1)} fusion(bf16[4,4,64,128]{3,2,1,0:T(8,128)(2,1)S(1)} %all_gather.3), kind=kLoop, calls=%fused_computation | loop fusion | bytes 131072 | tf_op jit(solution)/shard_map/squeeze | solution.py:265
  7.9 2.3 %observe.1 = (bf16[80,1024]{1,0:T(8,128)(2,1)}, bf16[80,512]{1,0:T(8,128)(2,1)}, bf16[80,512]{1,0:T(8,128)(2,1)}) custom-call(s32[1]{0:T(128)} %bitcast.flag, s32[1]{0:T(128)S(6)} %copy.10.count, bf16[4,64,128]{2,1,0:T(8,128)(2,1)} %slice_bitcast_fusion.newest, f32[4,1024]{1,0:T(4,128)} %coef.1, s32[1,1024]{1,0:T(1,128)} %bitcast.6, f32[1,1024]{1,0:T(1,128)} %bitcast.7, ...), custom_call_target="tpu_custom_call" | custom-call | tf_op jit(solution)/shard_map/observe/pallas_call | solution.py:209
  10.2 10.6 %collective-permute-start = (bf16[80,512]{1,0:T(8,128)(2,1)}, bf16[80,512]{1,0:T(8,128)(2,1)S(1)}, u32[]{:S(2)}, u32[]{:S(2)}) collective-permute-start(bf16[80,512]{1,0:T(8,128)(2,1)} %get-tuple-element.9), channel_id=1, source_target_pairs={{4,8},{8,4},{12,16},{16,12},{20,24},{24,20},{28,32},{32,28},{36,40... | collective-permute-start | bytes 245768 | tf_op jit(solution)/shard_map/ppermute | solution.py:269
  20.8 0.1 collective-permute-start.1
  20.9 3.0 %collective-permute-done.first = bf16[80,512]{1,0:T(8,128)(2,1)S(1)} collective-permute-done((bf16[80,512]{1,0:T(8,128)(2,1)}, bf16[80,512]{1,0:T(8,128)(2,1)S(1)}, u32[]{:S(2)}, u32[]{:S(2)}) %collective-permute-start) | collective-permute-done | bytes 81952 | tf_op jit(solution)/shard_map/ppermute | solution.py:269
  24.0 0.0 copy-start
  24.0 1.6 %collective-permute-done.1.second = bf16[80,512]{1,0:T(8,128)(2,1)S(1)} collective-permute-done((bf16[80,512]{1,0:T(8,128)(2,1)}, bf16[80,512]{1,0:T(8,128)(2,1)S(1)}, u32[]{:S(2)}, u32[]{:S(2)}) %collective-permute-start.1) | collective-permute-done | bytes 81952 | tf_op jit(solution)/shard_map/ppermute | solution.py:270
  25.6 0.0 copy-start.1
  25.6 0.0 copy-done
  25.6 0.6 %copy-done.1 = bf16[80,512]{1,0:T(8,128)(2,1)} copy-done((bf16[80,512]{1,0:T(8,128)(2,1)}, bf16[80,512]{1,0:T(8,128)(2,1)S(1)}, u32[]{:S(2)}) %copy-start.1) | copy-done | bytes 81944
  26.2 16.6 %solve.1 = bf16[2,4,64,128]{3,2,1,0:T(8,128)(2,1)} custom-call(s32[1]{0:T(128)} %bitcast.flag, s32[64,128]{1,0:T(8,128)} %index.1, bf16[80,1024]{1,0:T(8,128)(2,1)} %get-tuple-element.8.own, bf16[80,512]{1,0:T(8,128)(2,1)} %copy-done, bf16[80,512]{1,0:T(8,128)(2,1)} %copy-done.1, f32[64,128]{1,0:T(8,128)} %local.1, bf16[2,4,64,128]{3,2,1,0:T(8,128)(2,1)} %prior.1), custom_call_target="tpu_custom_call" | custom-call | tf_op jit(solution)/shard_map/solve/pallas_call | solution.py:221
Async XLA Ops:
  0.7 0.8 %slice-start = ((bf16[2,4,64,128]{3,2,1,0:T(8,128)(2,1)}), bf16[1,4,64,128]{3,2,1,0:T(8,128)(2,1)S(1)}, s32[]{:S(2)}) async-start(bf16[2,4,64,128]{3,2,1,0:T(8,128)(2,1)} %prior.1), calls=%async_computation | async-start | bytes 131072 | tf_op jit(solution)/shard_map/slice | solution.py:265
  10.2 13.8 %collective-permute-start = (bf16[80,512]{1,0:T(8,128)(2,1)}, bf16[80,512]{1,0:T(8,128)(2,1)S(1)}, u32[]{:S(2)}, u32[]{:S(2)}) collective-permute-start(bf16[80,512]{1,0:T(8,128)(2,1)} %get-tuple-element.9), channel_id=1, source_target_pairs={{4,8},{8,4},{12,16},{16,12},{20,24},{24,20},{28,32},{32,28},{36,40... | collective-permute-start | bytes 245768 | tf_op jit(solution)/shard_map/ppermute | solution.py:269
  20.8 4.7 %collective-permute-start.1 = (bf16[80,512]{1,0:T(8,128)(2,1)}, bf16[80,512]{1,0:T(8,128)(2,1)S(1)}, u32[]{:S(2)}, u32[]{:S(2)}) collective-permute-start(bf16[80,512]{1,0:T(8,128)(2,1)} %get-tuple-element.10), channel_id=1, source_target_pairs={{0,4},{4,0},{8,12},{12,8},{16,20},{20,16},{24,28},{28,24},{32,36},... | collective-permute-start | bytes 245768 | tf_op jit(solution)/shard_map/ppermute | solution.py:270
  24.0 1.6 %copy-start = (bf16[80,512]{1,0:T(8,128)(2,1)}, bf16[80,512]{1,0:T(8,128)(2,1)S(1)}, u32[]{:S(2)}) copy-start(bf16[80,512]{1,0:T(8,128)(2,1)S(1)} %collective-permute-done.first) | copy-start | bytes 245764
  25.6 0.6 %copy-start.1 = (bf16[80,512]{1,0:T(8,128)(2,1)}, bf16[80,512]{1,0:T(8,128)(2,1)S(1)}, u32[]{:S(2)}) copy-start(bf16[80,512]{1,0:T(8,128)(2,1)S(1)} %collective-permute-done.1.second) | copy-start | bytes 245764

commit v3 on v2

--- a/solution.py
+++ b/solution.py
@@ -1,5 +1,3 @@
-import functools
-
 import jax
 import jax.numpy as jnp
 from jax import lax
@@ -7,12 +5,15 @@
 from jax.experimental.pallas import tpu as pltpu
 from jax.sharding import PartitionSpec as P
 
+
 K = 64
 HALF = 64
 ROWS = 80
 UA = 16
 UC = 16
 INTERPRET = False
+OBSERVE_BYTES = 12 << 20
+SOLVE_BYTES = 24 << 20
 F32 = jnp.float32
 BF16 = jnp.bfloat16
 
@@ -27,11 +28,11 @@
 
 def observe_kernel(flag, count, newest, coef, column, value, weight, lists, own, first, second):
     slots = column.shape[1]
-    spec = newest.shape[0]
+    lags, spec = newest.shape[0], newest.shape[1]
     halo = lists.shape[1]
     hot = lax.broadcasted_iota(jnp.int32, (128, slots), 0) == column[...]
     hot = jnp.where(hot, 1.0, 0.0).astype(BF16)
-    picked = dot(newest[...].reshape(spec * K, 128), hot)
+    picked = dot(newest[lags - 1].reshape(spec * K, 128), hot)
     hx = coef[0:1, :] * picked[0:K]
     for s in range(1, spec):
         hx = hx + coef[s : s + 1, :] * picked[s * K : (s + 1) * K]
@@ -211,6 +212,7 @@
         out_shape=[jax.ShapeDtypeStruct(s, BF16) for s in shapes],
         in_specs=[smem(), smem()] + [vmem()] * 6,
         out_specs=[vmem()] * 3,
+        compiler_params=pltpu.CompilerParams(vmem_limit_bytes=OBSERVE_BYTES),
         interpret=INTERPRET,
         name="observe",
     )(flag, count, newest, coef, column[None], value[None], weight[None], lists)
@@ -236,6 +238,7 @@
             pltpu.VMEM((8, 128), F32),
             pltpu.VMEM((HALF, 128), F32),
         ],
+        compiler_params=pltpu.CompilerParams(vmem_limit_bytes=SOLVE_BYTES),
         interpret=INTERPRET,
         name="solve",
     )(flag, index, own, first, second, local, prior)
@@ -259,15 +262,14 @@
     neighbours,
     localization,
 ):
-    lags = lax.axis_size("lag")
     tiles = lax.axis_size("space")
     flag = (lax.axis_index("space") % 2)[None].astype(jnp.int32)
-    newest = lax.all_gather(prior[-1], "lag")[lags - 1]
+    newest = lax.all_gather(prior[-1], "lag")
     own, first, second = observe(
         flag, obs_count, newest, obs_coef, obs_column, obs_value, obs_weight, halo_lists
     )
+    second = lax.ppermute(second, "space", swaps(tiles, 0))
     first = lax.ppermute(first, "space", swaps(tiles, 1))
-    second = lax.ppermute(second, "space", swaps(tiles, 0))
     return solve(flag, neighbours, own, first, second, localization, prior)
 
 

time: 43 us -> 40.7 us (0.947)
  Pallas kernels: 18.9 us -> 17.1 us
  local copies, waits for them, and re-layouts: 2.1 us -> 1.54 us
    pallas_call x1, Pallas kernels: 2.31 us -> 0.78 us  [observe(): pl.pallas_call(observe_kernel, out_shape=[jax.ShapeDtypeStruct(s, BF16) f...]
    squeeze x1 -> x0, local copies, waits for them, and re-layouts: 0.63 us -> none  [body(): newest = lax.all_gather(prior[-1], 'lag')[lags - 1]]
where the time goes in v3:
time: 40.7 us; the launch traced here: 40.4 us
  Pallas kernels  17.1 us (42%)
  starting transfers between devices  10.7 us (26%)
  blocking collectives  5.89 us (14%)
  waiting for transfers between devices  4.43 us (11%)
  local copies, waits for them, and re-layouts  1.54 us (4%)
  between operations  0.71 us (2%)
    pallas_call x1, Pallas kernels, solve(): pl.pallas_call(solve_kernel, out_shape=jax.ShapeDtypeStruct(prior.shape,...  16.3 us
    ppermute x1, starting transfers between devices, body(): first = lax.ppermute(first, 'space', swaps(tiles, 1))  10.6 us
    all_gather x1, blocking collectives, body(): newest = lax.all_gather(prior[-1], 'lag')  5.89 us
    ppermute x1, waiting for transfers between devices, body(): first = lax.ppermute(first, 'space', swaps(tiles, 1))  2.84 us
    ppermute x1, waiting for transfers between devices, body(): second = lax.ppermute(second, 'space', swaps(tiles, 0))  1.59 us
    slice x2, local copies, waits for them, and re-layouts, body(): newest = lax.all_gather(prior[-1], 'lag')  0.84 us
  transfers between devices with their start and end apart: 2, of which 2 were waited for; matrix products, arithmetic and copies ran while one was open for 0% of the time, Pallas kernels for 0%

profile of v3, /device:TPU:24, one launch (start us, length us, event | category | flops | bytes accessed | tf_op | source)
XLA Modules:
  0.0 40.4 jit_solution(13462091567659036276)
XLA Ops:
  0.7 0.0 slice-start
  0.7 0.8 %slice-done = bf16[1,4,64,128]{3,2,1,0:T(8,128)(2,1)S(1)} async-done(((bf16[2,4,64,128]{3,2,1,0:T(8,128)(2,1)}), bf16[1,4,64,128]{3,2,1,0:T(8,128)(2,1)S(1)}, s32[]{:S(2)}) %slice-start) | async-done | bytes 65560 | tf_op jit(solution)/shard_map/slice | solution.py:267
  1.5 0.0 copy-start.3
  1.5 0.0 copy-start.6
  1.5 0.0 copy-start.7
  1.5 5.9 %all_gather.3.newest = bf16[4,4,64,128]{3,2,1,0:T(8,128)(2,1)S(1)} all-gather(bf16[1,4,64,128]{3,2,1,0:T(8,128)(2,1)S(1)} %slice-done), channel_id=1, replica_groups=mesh['space'=64,'lag'=4] {'lag'}, dimensions={0}, use_global_device_ids=true | all-gather | bytes 327680 | tf_op jit(solution)/shard_map/all_gather | solution.py:267
  7.4 0.0 copy-start.5
  7.4 0.0 copy-start.4
  7.4 0.0 copy-done.3
  7.4 0.0 copy-done.6
  7.4 0.0 copy-done.7
  7.4 0.7 %copy-done.5 = f32[1024]{0:T(1024)S(1)} copy-done((f32[1024]{0:T(1024)S(1)}, f32[1024]{0:T(1024)}, u32[]{:S(2)}) %copy-start.5) | copy-done | bytes 4120
  8.1 0.0 copy-done.4
  8.1 0.0 copy-start
  8.1 0.0 copy-start.1
  8.1 0.8 %observe.1 = (bf16[80,1024]{1,0:T(8,128)(2,1)S(1)}, bf16[80,512]{1,0:T(8,128)(2,1)S(1)}, bf16[80,512]{1,0:T(8,128)(2,1)S(1)}) custom-call(s32[1]{0:T(128)} %bitcast.flag, s32[1]{0:T(128)S(6)} %copy.10.count, bf16[4,4,64,128]{3,2,1,0:T(8,128)(2,1)S(1)} %all_gather.3.newest, f32[4,1024]{1,0:T(4,128)S(1)} %copy-done.3, s32[1,1024]{1,0:T(1,128)S(1)} %bitcast.4, ...), custom_call_target="tpu_custom_call" | custom-call | tf_op jit(solution)/shard_map/observe/pallas_call | solution.py:210
  8.9 10.6 %collective-permute-start = (bf16[80,512]{1,0:T(8,128)(2,1)S(1)}, bf16[80,512]{1,0:T(8,128)(2,1)S(1)}, u32[]{:S(2)}, u32[]{:S(2)}) collective-permute-start(bf16[80,512]{1,0:T(8,128)(2,1)S(1)} %get-tuple-element.9), channel_id=1, source_target_pairs={{4,8},{8,4},{12,16},{16,12},{20,24},{24,20},{28,32},{32,28},{36,40... | collective-permute-start | bytes 245768 | tf_op jit(solution)/shard_map/ppermute | solution.py:272
  19.5 0.1 collective-permute-start.1
  19.6 2.8 %collective-permute-done.first = bf16[80,512]{1,0:T(8,128)(2,1)S(1)} collective-permute-done((bf16[80,512]{1,0:T(8,128)(2,1)S(1)}, bf16[80,512]{1,0:T(8,128)(2,1)S(1)}, u32[]{:S(2)}, u32[]{:S(2)}) %collective-permute-start) | collective-permute-done | bytes 81952 | tf_op jit(solution)/shard_map/ppermute | solution.py:272
  22.5 1.6 %collective-permute-done.1.second = bf16[80,512]{1,0:T(8,128)(2,1)S(1)} collective-permute-done((bf16[80,512]{1,0:T(8,128)(2,1)S(1)}, bf16[80,512]{1,0:T(8,128)(2,1)S(1)}, u32[]{:S(2)}, u32[]{:S(2)}) %collective-permute-start.1) | collective-permute-done | bytes 81952 | tf_op jit(solution)/shard_map/ppermute | solution.py:271
  24.1 0.0 copy-done
  24.1 0.0 copy-done.1
  24.1 0.0 copy-done.2
  24.1 16.3 %solve.1 = bf16[2,4,64,128]{3,2,1,0:T(8,128)(2,1)} custom-call(s32[1]{0:T(128)} %bitcast.flag, s32[64,128]{1,0:T(8,128)S(1)} %copy-done.1, bf16[80,1024]{1,0:T(8,128)(2,1)S(1)} %get-tuple-element.8.own, bf16[80,512]{1,0:T(8,128)(2,1)S(1)} %collective-permute-done.first, bf16[80,512]{1,0:T(8,128)(2,1)S(1)} %collective-permute-done.1.second, ...), custom_call_target="tpu_custom_call" | custom-call | tf_op jit(solution)/shard_map/solve/pallas_call | solution.py:223
  (1 shorter events, 0.0 us)
Async XLA Ops:
  0.7 0.8 %slice-start = ((bf16[2,4,64,128]{3,2,1,0:T(8,128)(2,1)}), bf16[1,4,64,128]{3,2,1,0:T(8,128)(2,1)S(1)}, s32[]{:S(2)}) async-start(bf16[2,4,64,128]{3,2,1,0:T(8,128)(2,1)} %prior.1), calls=%async_computation | async-start | bytes 131072 | tf_op jit(solution)/shard_map/slice | solution.py:267
  1.5 5.9 %copy-start.3 = (f32[4,1024]{1,0:T(4,128)S(1)}, f32[4,1024]{1,0:T(4,128)}, u32[]{:S(2)}) copy-start(f32[4,1024]{1,0:T(4,128)} %coef.1) | copy-start | bytes 49156
  1.5 5.9 %copy-start.6 = (f32[1024]{0:T(1024)S(1)}, f32[1024]{0:T(1024)}, u32[]{:S(2)}) copy-start(f32[1024]{0:T(1024)} %param.11) | copy-start | bytes 12292
  1.5 5.9 %copy-start.7 = (s32[2,512]{1,0:T(2,128)S(1)}, s32[2,512]{1,0:T(2,128)}, u32[]{:S(2)}) copy-start(s32[2,512]{1,0:T(2,128)} %lists.1) | copy-start | bytes 12292
  7.4 0.7 %copy-start.5 = (f32[1024]{0:T(1024)S(1)}, f32[1024]{0:T(1024)}, u32[]{:S(2)}) copy-start(f32[1024]{0:T(1024)} %param.10) | copy-start | bytes 12292
  7.4 0.7 %copy-start.4 = (s32[1024]{0:T(1024)S(1)}, s32[1024]{0:T(1024)}, u32[]{:S(2)}) copy-start(s32[1024]{0:T(1024)} %param.13) | copy-start | bytes 12292
  8.1 16.0 %copy-start = (bf16[2,4,64,128]{3,2,1,0:T(8,128)(2,1)S(1)}, bf16[2,4,64,128]{3,2,1,0:T(8,128)(2,1)}, u32[]{:S(2)}) copy-start(bf16[2,4,64,128]{3,2,1,0:T(8,128)(2,1)} %prior.1) | copy-start | bytes 393220
  8.1 16.0 %copy-start.1 = (s32[64,128]{1,0:T(8,128)S(1)}, s32[64,128]{1,0:T(8,128)}, u32[]{:S(2)}) copy-start(s32[64,128]{1,0:T(8,128)} %index.1) | copy-start | bytes 98308
  8.1 16.0 %copy-start.2 = (f32[64,128]{1,0:T(8,128)S(1)}, f32[64,128]{1,0:T(8,128)}, u32[]{:S(2)}) copy-start(f32[64,128]{1,0:T(8,128)} %local.1) | copy-start | bytes 98308
  8.9 13.6 %collective-permute-start = (bf16[80,512]{1,0:T(8,128)(2,1)S(1)}, bf16[80,512]{1,0:T(8,128)(2,1)S(1)}, u32[]{:S(2)}, u32[]{:S(2)}) collective-permute-start(bf16[80,512]{1,0:T(8,128)(2,1)S(1)} %get-tuple-element.9), channel_id=1, source_target_pairs={{4,8},{8,4},{12,16},{16,12},{20,24},{24,20},{28,32},{32,28},{36,40... | collective-permute-start | bytes 245768 | tf_op jit(solution)/shard_map/ppermute | solution.py:272
  19.5 4.5 %collective-permute-start.1 = (bf16[80,512]{1,0:T(8,128)(2,1)S(1)}, bf16[80,512]{1,0:T(8,128)(2,1)S(1)}, u32[]{:S(2)}, u32[]{:S(2)}) collective-permute-start(bf16[80,512]{1,0:T(8,128)(2,1)S(1)} %get-tuple-element.10), channel_id=1, source_target_pairs={{0,4},{4,0},{8,12},{12,8},{16,20},{20,16},{24,28},{28,24},{32,36},... | collective-permute-start | bytes 245768 | tf_op jit(solution)/shard_map/ppermute | solution.py:271

commit v4 on v3

--- a/solution.py
+++ b/solution.py
@@ -9,8 +9,8 @@
 K = 64
 HALF = 64
 ROWS = 80
-UA = 16
-UC = 16
+UA = 32
+UC = 32
 INTERPRET = False
 OBSERVE_BYTES = 12 << 20
 SOLVE_BYTES = 24 << 20
@@ -74,28 +74,22 @@
 
 def solve_kernel(
     flag, index, own, first, second, local, prior, out,
-    table_a, table_b, rows, matrix, squares, factors, pd, mixed, shift, means, weights,
+    matrix, squares, factors, pd, mixed, shift, means, weights, lows, codes,
 ):
     lags, spec = prior.shape[0], prior.shape[1]
-    slots, halo = own.shape[1], first.shape[1]
+    halo = first.shape[1]
     odd = flag[0]
     left = lanes_of((HALF, 128)) < HALF
 
-    def put(source, offset, block):
-        piece = source[:, block * 128 : (block + 1) * 128].astype(F32)
-        piece = jnp.concatenate([piece, jnp.zeros((128 - ROWS, 128), F32)], axis=0).T
-        at = pl.multiple_of(offset + block * 128, 128)
-        table_a[pl.ds(at, 128), :] = piece
-        table_b[pl.ds(at, 128), :] = pltpu.roll(piece, HALF, 1)
-
-    for b in range(slots // 128):
-        put(own, 0, b)
-    for b in range(halo // 128):
-        put(first, slots + odd * halo, b)
-        put(second, slots + (1 - odd) * halo, b)
-
-    twice = jnp.concatenate([local[...], local[...]], axis=0).T
-    weights[...] = jnp.where(left, twice[0:HALF], twice[HALF:])
+    def beside(values):
+        twice = jnp.concatenate([values, values], axis=0).T
+        return jnp.where(left, twice[0:HALF], twice[HALF:])
+
+    weights[...] = beside(local[...])
+    places = beside(index[...].astype(F32)).astype(jnp.int32)
+    block = places >> 9
+    lows[...] = (places & 511).astype(F32)
+    codes[...] = jnp.where(block >= 2, block ^ odd, block)
 
     def rank(pair):
         lag, s = pair // spec, pair % spec
@@ -115,32 +109,44 @@
     leftb = lanes_of((HALF, 128)) < HALF
     ones = block_diagonal(jnp.ones((HALF, 128), F32), left).astype(BF16)
 
+    stacked = jnp.concatenate(
+        [own[:, 0:halo], own[:, halo:], first[...], second[...]], axis=0
+    )
+    counts = lax.broadcasted_iota(jnp.int32, (256, 256), 0).astype(F32).astype(BF16)
+
+    def pick(q):
+        low = jnp.concatenate([lows[pl.ds(q, 1), :], lows[pl.ds(q + 1, 1), :]], axis=1)
+        code = jnp.concatenate([codes[pl.ds(q, 1), :], codes[pl.ds(q + 1, 1), :]], axis=1)
+        hot = [
+            jnp.where(counts == (low - 256.0 * h).astype(BF16), 1.0, 0.0).astype(BF16)
+            for h in range(halo // 256)
+        ]
+        found = dot(stacked, jnp.concatenate(hot, axis=0))
+        total = found[0:ROWS]
+        for b in range(1, 4):
+            total = jnp.where(code == b, found[b * ROWS : (b + 1) * ROWS], total)
+        return total[:, 0:128], total[:, 128:]
+
     @pl.loop(0, HALF // UA)
     def _(step):
         qs = [step * UA + u for u in range(UA)]
-        for u, q in enumerate(qs):
-            for n in range(HALF):
-                rows[u, n : n + 1, :] = table_a[pl.ds(index[n, q], 1), :]
-                rows[u, HALF + n : HALF + n + 1, :] = table_b[pl.ds(index[n, q + HALF], 1), :]
+        picked = []
+        for q in qs[::2]:
+            picked += pick(q)
         lefts, diagonals = [], []
-        top = left[0:1]
-        zero = jnp.zeros((HALF, 128), F32)
-        for u, q in enumerate(qs):
-            found = rows[u]
-            across = found.T
-            gathered = jnp.where(left, across[0:HALF], across[HALF:])
-            info0 = jnp.where(top, across[HALF : HALF + 1], across[0:1])
-            info1 = jnp.where(top, across[HALF + 1 : HALF + 2], across[1:2])
-            scaled = weights[pl.ds(q, 1), :] * info0
+        for q, found in zip(qs, picked):
+            gathered = found[0:HALF]
+            scaled = weights[pl.ds(q, 1), :] * found[HALF : HALF + 1]
             weighted = (gathered * scaled).astype(BF16)
-            pull = scaled * info1
+            pull = scaled * found[HALF + 1 : HALF + 2]
             pull_high = pull.astype(BF16).astype(F32)
             extra = jnp.concatenate([pull_high, pull - pull_high, jnp.zeros((14, 128), F32)], axis=0)
             lefts.append(jnp.concatenate([weighted, extra.astype(BF16)], axis=0))
-            diagonals.append(jnp.concatenate(
-                [jnp.where(left, found[0:HALF], zero), jnp.where(left, zero, found[HALF:])], axis=0
-            ).astype(BF16))
-        products = [dot(l, d) for l, d in zip(lefts, diagonals)]
+            diagonals.append(block_diagonal(gathered.astype(BF16), leftb))
+        products = [
+            lax.dot_general(l, d, (((1,), (1,)), ((), ())), preferred_element_type=F32)
+            for l, d in zip(lefts, diagonals)
+        ]
         for q, product in zip(qs, products):
             full = eye + product[0:HALF] * (1.0 / (K - 1))
             matrix[q] = full
@@ -219,16 +225,12 @@
 
 
 def solve(flag, index, own, first, second, local, prior):
-    positions = own.shape[1] + 2 * first.shape[1]
     return pl.pallas_call(
         solve_kernel,
         out_shape=jax.ShapeDtypeStruct(prior.shape, BF16),
-        in_specs=[smem(), smem()] + [vmem()] * 5,
+        in_specs=[smem()] + [vmem()] * 6,
         out_specs=vmem(),
         scratch_shapes=[
-            pltpu.VMEM((positions, 128), F32),
-            pltpu.VMEM((positions, 128), F32),
-            pltpu.VMEM((UA, 128, 128), F32),
             pltpu.VMEM((HALF, HALF, 128), F32),
             pltpu.VMEM((HALF, 128), F32),
             pltpu.VMEM((HALF, 128), F32),
@@ -237,6 +239,8 @@
             pltpu.VMEM((HALF * 8, 128), F32),
             pltpu.VMEM((8, 128), F32),
             pltpu.VMEM((HALF, 128), F32),
+            pltpu.VMEM((HALF, 128), F32),
+            pltpu.VMEM((HALF, 128), jnp.int32),
         ],
         compiler_params=pltpu.CompilerParams(vmem_limit_bytes=SOLVE_BYTES),
         interpret=INTERPRET,

time: 40.7 us -> 32.9 us (0.81)
  Pallas kernels: 17.1 us -> 9.4 us
    pallas_call x1, Pallas kernels: 16.3 us -> 8.61 us  [solve(): pl.pallas_call(solve_kernel, out_shape=jax.ShapeDtypeStruct(prior.shape,...]
where the time goes in v4:
time: 32.9 us; the launch traced here: 32.7 us
  starting transfers between devices  10.7 us (33%)
  Pallas kernels  9.4 us (29%)
  blocking collectives  5.89 us (18%)
  waiting for transfers between devices  4.43 us (13%)
  local copies, waits for them, and re-layouts  1.54 us (5%)
  between operations  0.71 us (2%)
    ppermute x1, starting transfers between devices, body(): first = lax.ppermute(first, 'space', swaps(tiles, 1))  10.6 us
    pallas_call x1, Pallas kernels, solve(): pl.pallas_call(solve_kernel, out_shape=jax.ShapeDtypeStruct(prior.shape,...  8.61 us
    all_gather x1, blocking collectives, body(): newest = lax.all_gather(prior[-1], 'lag')  5.89 us
    ppermute x1, waiting for transfers between devices, body(): first = lax.ppermute(first, 'space', swaps(tiles, 1))  2.84 us
    ppermute x1, waiting for transfers between devices, body(): second = lax.ppermute(second, 'space', swaps(tiles, 0))  1.59 us
    slice x2, local copies, waits for them, and re-layouts, body(): newest = lax.all_gather(prior[-1], 'lag')  0.84 us
    pallas_call x1, Pallas kernels, observe(): pl.pallas_call(observe_kernel, out_shape=[jax.ShapeDtypeStruct(s, BF16) f...  0.78 us
    unnamed x16, local copies, waits for them, and re-layouts  0.71 us
  transfers between devices with their start and end apart: 2, of which 2 were waited for; matrix products, arithmetic and copies ran while one was open for 0% of the time, Pallas kernels for 0%

profile of v4, /device:TPU:24, one launch (start us, length us, event | category | flops | bytes accessed | tf_op | source)
XLA Modules:
  0.0 32.7 jit_solution(7711749741321754222)
XLA Ops:
  0.7 0.0 slice-start
  0.7 0.8 %slice-done = bf16[1,4,64,128]{3,2,1,0:T(8,128)(2,1)S(1)} async-done(((bf16[2,4,64,128]{3,2,1,0:T(8,128)(2,1)}), bf16[1,4,64,128]{3,2,1,0:T(8,128)(2,1)S(1)}, s32[]{:S(2)}) %slice-start) | async-done | bytes 65560 | tf_op jit(solution)/shard_map/slice | solution.py:271
  1.5 0.0 copy-start.3
  1.5 0.0 copy-start.6
  1.5 0.0 copy-start.7
  1.5 5.9 %all_gather.3.newest = bf16[4,4,64,128]{3,2,1,0:T(8,128)(2,1)S(1)} all-gather(bf16[1,4,64,128]{3,2,1,0:T(8,128)(2,1)S(1)} %slice-done), channel_id=1, replica_groups=mesh['space'=64,'lag'=4] {'lag'}, dimensions={0}, use_global_device_ids=true | all-gather | bytes 327680 | tf_op jit(solution)/shard_map/all_gather | solution.py:271
  7.4 0.0 copy-start.5
  7.4 0.0 copy-start.4
  7.4 0.0 copy-done.3
  7.4 0.0 copy-done.6
  7.4 0.0 copy-done.7
  7.4 0.7 %copy-done.5 = f32[1024]{0:T(1024)S(1)} copy-done((f32[1024]{0:T(1024)S(1)}, f32[1024]{0:T(1024)}, u32[]{:S(2)}) %copy-start.5) | copy-done | bytes 4120
  8.1 0.0 copy-done.4
  8.1 0.0 copy-start
  8.1 0.0 copy-start.1
  8.1 0.8 %observe.1 = (bf16[80,1024]{1,0:T(8,128)(2,1)S(1)}, bf16[80,512]{1,0:T(8,128)(2,1)S(1)}, bf16[80,512]{1,0:T(8,128)(2,1)S(1)}) custom-call(s32[1]{0:T(128)} %bitcast.flag, s32[1]{0:T(128)S(6)} %copy.10.count, bf16[4,4,64,128]{3,2,1,0:T(8,128)(2,1)S(1)} %all_gather.3.newest, f32[4,1024]{1,0:T(4,128)S(1)} %copy-done.3, s32[1,1024]{1,0:T(1,128)S(1)} %bitcast.4, ...), custom_call_target="tpu_custom_call" | custom-call | tf_op jit(solution)/shard_map/observe/pallas_call | solution.py:216
  8.9 10.6 %collective-permute-start = (bf16[80,512]{1,0:T(8,128)(2,1)S(1)}, bf16[80,512]{1,0:T(8,128)(2,1)S(1)}, u32[]{:S(2)}, u32[]{:S(2)}) collective-permute-start(bf16[80,512]{1,0:T(8,128)(2,1)S(1)} %get-tuple-element.9), channel_id=1, source_target_pairs={{4,8},{8,4},{12,16},{16,12},{20,24},{24,20},{28,32},{32,28},{36,40... | collective-permute-start | bytes 245768 | tf_op jit(solution)/shard_map/ppermute | solution.py:276
  19.5 0.1 collective-permute-start.1
  19.6 2.8 %collective-permute-done.first = bf16[80,512]{1,0:T(8,128)(2,1)S(1)} collective-permute-done((bf16[80,512]{1,0:T(8,128)(2,1)S(1)}, bf16[80,512]{1,0:T(8,128)(2,1)S(1)}, u32[]{:S(2)}, u32[]{:S(2)}) %collective-permute-start) | collective-permute-done | bytes 81952 | tf_op jit(solution)/shard_map/ppermute | solution.py:276
  22.5 1.6 %collective-permute-done.1.second = bf16[80,512]{1,0:T(8,128)(2,1)S(1)} collective-permute-done((bf16[80,512]{1,0:T(8,128)(2,1)S(1)}, bf16[80,512]{1,0:T(8,128)(2,1)S(1)}, u32[]{:S(2)}, u32[]{:S(2)}) %collective-permute-start.1) | collective-permute-done | bytes 81952 | tf_op jit(solution)/shard_map/ppermute | solution.py:275
  24.1 0.0 copy-done
  24.1 0.0 copy-done.1
  24.1 0.0 copy-done.2
  24.1 8.6 %solve.1 = bf16[2,4,64,128]{3,2,1,0:T(8,128)(2,1)} custom-call(s32[1]{0:T(128)} %bitcast.flag, s32[64,128]{1,0:T(8,128)S(1)} %copy-done.1, bf16[80,1024]{1,0:T(8,128)(2,1)S(1)} %get-tuple-element.8.own, bf16[80,512]{1,0:T(8,128)(2,1)S(1)} %collective-permute-done.first, bf16[80,512]{1,0:T(8,128)(2,1)S(1)} %collective-permute-done.1.second, ...), custom_call_target="tpu_custom_call" | custom-call | tf_op jit(solution)/shard_map/solve/pallas_call | solution.py:228
  (1 shorter events, 0.0 us)
Async XLA Ops:
  0.7 0.8 %slice-start = ((bf16[2,4,64,128]{3,2,1,0:T(8,128)(2,1)}), bf16[1,4,64,128]{3,2,1,0:T(8,128)(2,1)S(1)}, s32[]{:S(2)}) async-start(bf16[2,4,64,128]{3,2,1,0:T(8,128)(2,1)} %prior.1), calls=%async_computation | async-start | bytes 131072 | tf_op jit(solution)/shard_map/slice | solution.py:271
  1.5 5.9 %copy-start.3 = (f32[4,1024]{1,0:T(4,128)S(1)}, f32[4,1024]{1,0:T(4,128)}, u32[]{:S(2)}) copy-start(f32[4,1024]{1,0:T(4,128)} %coef.1) | copy-start | bytes 49156
  1.5 5.9 %copy-start.6 = (f32[1024]{0:T(1024)S(1)}, f32[1024]{0:T(1024)}, u32[]{:S(2)}) copy-start(f32[1024]{0:T(1024)} %param.11) | copy-start | bytes 12292
  1.5 5.9 %copy-start.7 = (s32[2,512]{1,0:T(2,128)S(1)}, s32[2,512]{1,0:T(2,128)}, u32[]{:S(2)}) copy-start(s32[2,512]{1,0:T(2,128)} %lists.1) | copy-start | bytes 12292
  7.4 0.7 %copy-start.5 = (f32[1024]{0:T(1024)S(1)}, f32[1024]{0:T(1024)}, u32[]{:S(2)}) copy-start(f32[1024]{0:T(1024)} %param.10) | copy-start | bytes 12292
  7.4 0.7 %copy-start.4 = (s32[1024]{0:T(1024)S(1)}, s32[1024]{0:T(1024)}, u32[]{:S(2)}) copy-start(s32[1024]{0:T(1024)} %param.13) | copy-start | bytes 12292
  8.1 16.0 %copy-start = (bf16[2,4,64,128]{3,2,1,0:T(8,128)(2,1)S(1)}, bf16[2,4,64,128]{3,2,1,0:T(8,128)(2,1)}, u32[]{:S(2)}) copy-start(bf16[2,4,64,128]{3,2,1,0:T(8,128)(2,1)} %prior.1) | copy-start | bytes 393220
  8.1 16.0 %copy-start.1 = (s32[64,128]{1,0:T(8,128)S(1)}, s32[64,128]{1,0:T(8,128)}, u32[]{:S(2)}) copy-start(s32[64,128]{1,0:T(8,128)} %index.1) | copy-start | bytes 98308
  8.1 16.0 %copy-start.2 = (f32[64,128]{1,0:T(8,128)S(1)}, f32[64,128]{1,0:T(8,128)}, u32[]{:S(2)}) copy-start(f32[64,128]{1,0:T(8,128)} %local.1) | copy-start | bytes 98308
  8.9 13.6 %collective-permute-start = (bf16[80,512]{1,0:T(8,128)(2,1)S(1)}, bf16[80,512]{1,0:T(8,128)(2,1)S(1)}, u32[]{:S(2)}, u32[]{:S(2)}) collective-permute-start(bf16[80,512]{1,0:T(8,128)(2,1)S(1)} %get-tuple-element.9), channel_id=1, source_target_pairs={{4,8},{8,4},{12,16},{16,12},{20,24},{24,20},{28,32},{32,28},{36,40... | collective-permute-start | bytes 245768 | tf_op jit(solution)/shard_map/ppermute | solution.py:276
  19.5 4.5 %collective-permute-start.1 = (bf16[80,512]{1,0:T(8,128)(2,1)S(1)}, bf16[80,512]{1,0:T(8,128)(2,1)S(1)}, u32[]{:S(2)}, u32[]{:S(2)}) collective-permute-start(bf16[80,512]{1,0:T(8,128)(2,1)S(1)} %get-tuple-element.10), channel_id=1, source_target_pairs={{0,4},{4,0},{8,12},{12,8},{16,20},{20,16},{24,28},{28,24},{32,36},... | collective-permute-start | bytes 245768 | tf_op jit(solution)/shard_map/ppermute | solution.py:275

commit v5 on v4

--- a/solution.py
+++ b/solution.py
@@ -26,7 +26,30 @@
     return jnp.dot(left, right, preferred_element_type=F32)
 
 
-def observe_kernel(flag, count, newest, coef, column, value, weight, lists, own, first, second):
+def stage_kernel(
+    prior, coef, column, value, weight, lists, count,
+    newest_out, coef_out, column_out, value_out, weight_out, lists_out, count_out,
+    scalar, sems,
+):
+    lags = prior.shape[0]
+    moves = (
+        (prior.at[pl.ds(lags - 1, 1)], newest_out),
+        (coef, coef_out),
+        (column, column_out),
+        (value, value_out),
+        (weight, weight_out),
+        (lists, lists_out),
+        (count, scalar),
+    )
+    copies = [pltpu.make_async_copy(a, b, sems.at[n]) for n, (a, b) in enumerate(moves)]
+    for copy in copies:
+        copy.start()
+    for copy in copies:
+        copy.wait()
+    count_out[...] = jnp.full((1, 128), scalar[0], jnp.int32)
+
+
+def observe_kernel(flag, newest, coef, column, value, weight, lists, count, own, first, second):
     slots = column.shape[1]
     lags, spec = newest.shape[0], newest.shape[1]
     halo = lists.shape[1]
@@ -37,7 +60,7 @@
     for s in range(1, spec):
         hx = hx + coef[s : s + 1, :] * picked[s * K : (s + 1) * K]
     mean = jnp.sum(hx, axis=0, keepdims=True) * (1.0 / K)
-    valid = jnp.where(lanes_of((1, slots)) < count[0], 1.0, 0.0)
+    valid = jnp.where(lanes_of((1, slots)) < count[:, 0:1], 1.0, 0.0)
     pert = (hx - mean) * valid
     info = jnp.concatenate(
         [weight[...] * valid, (value[...] - mean) * valid, jnp.zeros((ROWS - K - 2, slots), F32)],
@@ -72,13 +95,8 @@
     return jnp.concatenate([jnp.where(left, pair, zero), jnp.where(left, zero, pair)], axis=0)
 
 
-def solve_kernel(
-    flag, index, own, first, second, local, prior, out,
-    matrix, squares, factors, pd, mixed, shift, means, weights, lows, codes,
-):
+def prepare_kernel(flag, index, local, prior, pd, means, weights, lows, codes):
     lags, spec = prior.shape[0], prior.shape[1]
-    halo = first.shape[1]
-    odd = flag[0]
     left = lanes_of((HALF, 128)) < HALF
 
     def beside(values):
@@ -89,7 +107,7 @@
     places = beside(index[...].astype(F32)).astype(jnp.int32)
     block = places >> 9
     lows[...] = (places & 511).astype(F32)
-    codes[...] = jnp.where(block >= 2, block ^ odd, block)
+    codes[...] = jnp.where(block >= 2, block ^ flag[0], block)
 
     def rank(pair):
         lag, s = pair // spec, pair % spec
@@ -98,11 +116,20 @@
         means[pair : pair + 1, :] = mean
         return (values - mean).astype(BF16).astype(F32)
 
+    for pair in range(0, lags * spec, 2):
+        square = jnp.concatenate([rank(pair), rank(pair + 1)], axis=0).T
+        pd[pl.ds(pair, HALF, stride=8), :] = packed(square, True)
+        pd[pl.ds(pair + 1, HALF, stride=8), :] = packed(square, False)
+
+
+def solve_kernel(
+    own, first, second, pd, means, weights, lows, codes, out,
+    matrix, squares, factors, tails, mixed, shift,
+):
+    lags, spec = out.shape[0], out.shape[1]
     count = lags * spec
-    for pair in range(0, count, 2):
-        square = jnp.concatenate([rank(pair), rank(pair + 1)], axis=0).T
-        pd[pl.ds(pair, HALF, stride=16), :] = packed(square, True)
-        pd[pl.ds(pair + 1, HALF, stride=16), :] = packed(square, False)
+    halo = first.shape[1]
+    left = lanes_of((HALF, 128)) < HALF
 
     row = lax.broadcasted_iota(jnp.int32, (HALF, 128), 0)
     eye = jnp.where(row == (lanes_of((HALF, 128)) & (HALF - 1)), 1.0, 0.0)
@@ -154,7 +181,7 @@
             drive = product[HALF : HALF + 1] + product[HALF + 1 : HALF + 2]
             drive_low = drive - drive.astype(BF16).astype(F32)
             tail = jnp.concatenate([drive, drive_low, jnp.zeros((6, 128), F32)], axis=0)
-            pd[pl.ds(pl.multiple_of(q * 16 + 8, 8), 8), :] = tail
+            tails[pl.ds(pl.multiple_of(q * 8, 8), 8), :] = tail
 
     def half_sums(values):
         high = values.astype(BF16)
@@ -176,7 +203,8 @@
             z + 2.25 * eye - 2.4375 * a + 1.6875 * b
             for z, a, b in zip(zs, first_powers, second_powers)
         ]
-        sides = [pd[pl.ds(pl.multiple_of(q * 16, 16), 16), :].astype(BF16) for q in qs]
+        eights = [pl.ds(pl.multiple_of(q * 8, 8), 8) for q in qs]
+        sides = [jnp.concatenate([pd[at, :], tails[at, :]], axis=0).astype(BF16) for at in eights]
         products = [dot(p, block_diagonal(z.astype(BF16), leftb)) for p, z in zip(sides, zs)]
         for q, product in zip(qs, products):
             mix = product[0:8]
@@ -210,42 +238,80 @@
     return pl.BlockSpec(memory_space=pltpu.SMEM)
 
 
-def observe(flag, count, newest, coef, column, value, weight, lists):
-    slots, halo = column.shape[0], lists.shape[1]
+def anywhere():
+    return pl.BlockSpec(memory_space=pltpu.HBM)
+
+
+def stage(prior, coef, column, value, weight, lists, count):
+    shapes = [
+        jax.ShapeDtypeStruct((1, *prior.shape[1:]), prior.dtype),
+        *(jax.ShapeDtypeStruct(x.shape, x.dtype) for x in (coef, column, value, weight, lists)),
+        jax.ShapeDtypeStruct((1, 128), jnp.int32),
+    ]
+    return pl.pallas_call(
+        stage_kernel,
+        out_shape=shapes,
+        in_specs=[anywhere()] * 7,
+        out_specs=[vmem()] * 7,
+        scratch_shapes=[pltpu.SMEM((1,), jnp.int32), pltpu.SemaphoreType.DMA((7,))],
+        compiler_params=pltpu.CompilerParams(vmem_limit_bytes=OBSERVE_BYTES),
+        interpret=INTERPRET,
+        name="stage",
+    )(prior, coef, column, value, weight, lists, count)
+
+
+def observe(flag, newest, coef, column, value, weight, lists, count):
+    slots, halo = column.shape[1], lists.shape[1]
     shapes = [(ROWS, slots), (ROWS, halo), (ROWS, halo)]
     return pl.pallas_call(
         observe_kernel,
         out_shape=[jax.ShapeDtypeStruct(s, BF16) for s in shapes],
-        in_specs=[smem(), smem()] + [vmem()] * 6,
+        in_specs=[smem()] + [vmem()] * 7,
         out_specs=[vmem()] * 3,
         compiler_params=pltpu.CompilerParams(vmem_limit_bytes=OBSERVE_BYTES),
         interpret=INTERPRET,
         name="observe",
-    )(flag, count, newest, coef, column[None], value[None], weight[None], lists)
-
-
-def solve(flag, index, own, first, second, local, prior):
+    )(flag, newest, coef, column, value, weight, lists, count)
+
+
+def prepare(flag, index, local, prior):
+    ranks = prior.shape[0] * prior.shape[1]
+    shapes = [
+        jax.ShapeDtypeStruct((HALF * ranks, 128), F32),
+        jax.ShapeDtypeStruct((ranks, 128), F32),
+        jax.ShapeDtypeStruct((HALF, 128), F32),
+        jax.ShapeDtypeStruct((HALF, 128), F32),
+        jax.ShapeDtypeStruct((HALF, 128), jnp.int32),
+    ]
+    return pl.pallas_call(
+        prepare_kernel,
+        out_shape=shapes,
+        in_specs=[smem()] + [vmem()] * 3,
+        out_specs=[vmem()] * 5,
+        compiler_params=pltpu.CompilerParams(vmem_limit_bytes=OBSERVE_BYTES),
+        interpret=INTERPRET,
+        name="prepare",
+    )(flag, index, local, prior)
+
+
+def solve(own, first, second, pd, means, weights, lows, codes, shape):
     return pl.pallas_call(
         solve_kernel,
-        out_shape=jax.ShapeDtypeStruct(prior.shape, BF16),
-        in_specs=[smem()] + [vmem()] * 6,
+        out_shape=jax.ShapeDtypeStruct(shape, BF16),
+        in_specs=[vmem()] * 8,
         out_specs=vmem(),
         scratch_shapes=[
             pltpu.VMEM((HALF, HALF, 128), F32),
             pltpu.VMEM((HALF, 128), F32),
             pltpu.VMEM((HALF, 128), F32),
-            pltpu.VMEM((HALF * 16, 128), F32),
             pltpu.VMEM((HALF * 8, 128), F32),
             pltpu.VMEM((HALF * 8, 128), F32),
-            pltpu.VMEM((8, 128), F32),
-            pltpu.VMEM((HALF, 128), F32),
-            pltpu.VMEM((HALF, 128), F32),
-            pltpu.VMEM((HALF, 128), jnp.int32),
+            pltpu.VMEM((HALF * 8, 128), F32),
         ],
         compiler_params=pltpu.CompilerParams(vmem_limit_bytes=SOLVE_BYTES),
         interpret=INTERPRET,
         name="solve",
-    )(flag, index, own, first, second, local, prior)
+    )(own, first, second, pd, means, weights, lows, codes)
 
 
 def swaps(length, start):
@@ -268,13 +334,15 @@
 ):
     tiles = lax.axis_size("space")
     flag = (lax.axis_index("space") % 2)[None].astype(jnp.int32)
-    newest = lax.all_gather(prior[-1], "lag")
-    own, first, second = observe(
-        flag, obs_count, newest, obs_coef, obs_column, obs_value, obs_weight, halo_lists
-    )
+    newest, *staged = stage(
+        prior, obs_coef, obs_column[None], obs_value[None], obs_weight[None], halo_lists, obs_count
+    )
+    newest = lax.all_gather(newest, "lag", axis=0, tiled=True)
+    own, first, second = observe(flag, newest, *staged)
     second = lax.ppermute(second, "space", swaps(tiles, 0))
     first = lax.ppermute(first, "space", swaps(tiles, 1))
-    return solve(flag, neighbours, own, first, second, localization, prior)
+    ready = prepare(flag, neighbours, localization, prior)
+    return solve(own, first, second, *ready, prior.shape)
 
 
 def solution(mesh):

time: 32.9 us -> 32.6 us (level)
  Pallas kernels: 9.4 us -> 10.1 us
  local copies, waits for them, and re-layouts: 1.54 us -> 0.93 us
  waiting for transfers between devices: 4.43 us -> 4.04 us
    slice x2 -> x0, local copies, waits for them, and re-layouts: 0.84 us -> none  [body(): newest = lax.all_gather(prior[-1], 'lag')]
    pallas_call x1 -> x3, Pallas kernels: 8.61 us -> 9.34 us  [the longest x1 8.29 us: solve(): pl.pallas_call(solve_kernel, out_shape=jax.ShapeDtypeStruct(shape, BF16),...]
    ppermute x1, waiting for transfers between devices: 2.84 us -> 2.45 us  [body(): first = lax.ppermute(first, 'space', swaps(tiles, 1))]
    unnamed x16 -> x18, local copies, waits for them, and re-layouts: 0.71 us -> 0.93 us
  transfers between devices with their start and end apart: 2 -> 2, of which waited for: 2 -> 2; matrix products, arithmetic and copies ran while one was open for 0% -> 0% of each run, Pallas kernels for 0% -> 1%
where the time goes in v5:
time: 32.6 us; the launch traced here: 32.4 us
  starting transfers between devices  10.7 us (33%)
  Pallas kernels  10.1 us (31%)
  blocking collectives  5.78 us (18%)
  waiting for transfers between devices  4.04 us (12%)
  local copies, waits for them, and re-layouts  0.93 us (3%)
  between operations  0.84 us (3%)
    ppermute x1, starting transfers between devices, body(): first = lax.ppermute(first, 'space', swaps(tiles, 1))  10.6 us
    pallas_call x1, Pallas kernels, solve(): pl.pallas_call(solve_kernel, out_shape=jax.ShapeDtypeStruct(shape, BF16),...  8.29 us
    all_gather x1, blocking collectives, body(): newest = lax.all_gather(newest, 'lag', axis=0, tiled=True)  5.78 us
    ppermute x1, waiting for transfers between devices, body(): first = lax.ppermute(first, 'space', swaps(tiles, 1))  2.45 us
    ppermute x1, waiting for transfers between devices, body(): second = lax.ppermute(second, 'space', swaps(tiles, 0))  1.59 us
    unnamed x18, local copies, waits for them, and re-layouts  0.93 us
    pallas_call x1, Pallas kernels, observe(): pl.pallas_call(observe_kernel, out_shape=[jax.ShapeDtypeStruct(s, BF16) f...  0.77 us
    pallas_call x1, Pallas kernels, stage(): pl.pallas_call(stage_kernel, out_shape=shapes, in_specs=[anywhere()] * 7,...  0.7 us
  transfers between devices with their start and end apart: 2, of which 2 were waited for; matrix products, arithmetic and copies ran while one was open for 0% of the time, Pallas kernels for 1%

profile of v5, /device:TPU:24, one launch (start us, length us, event | category | flops | bytes accessed | tf_op | source)
XLA Modules:
  0.0 32.4 jit_solution(312035346598574057)
XLA Ops:
  0.0 0.0 copy-start.4
  0.0 0.0 copy-start.7
  0.0 0.0 copy-start.6
  0.0 0.0 copy-start.5
  0.7 0.0 copy-done.4
  0.7 0.0 copy-done.8
  0.8 0.0 copy-done.7
  0.8 0.0 copy-done.6
  0.8 0.0 copy-done.5
  0.8 0.0 copy-start
  0.8 0.9 %copy-done = bf16[2,4,64,128]{3,2,1,0:T(8,128)(2,1)S(1)} copy-done((bf16[2,4,64,128]{3,2,1,0:T(8,128)(2,1)S(1)}, bf16[2,4,64,128]{3,2,1,0:T(8,128)(2,1)}, u32[]{:S(2)}) %copy-start) | copy-done | bytes 131096
  1.7 0.7 %stage.1 = (bf16[1,4,64,128]{3,2,1,0:T(8,128)(2,1)S(1)}, f32[4,1024]{1,0:T(4,128)S(1)}, s32[1,1024]{1,0:T(1,128)S(1)}, f32[1,1024]{1,0:T(1,128)S(1)}, f32[1,1024...) custom-call(bf16[2,4,64,128]{3,2,1,0:T(8,128)(2,1)S(1)} %copy-done, f32[4,1024]{1,0:T(4,128)S(1)} %copy-done.4, ...), custom_call_target="tpu_custom_call" | custom-call | tf_op jit(solution)/shard_map/stage/pallas_call | solution.py:251
  2.4 5.8 %all_gather.3.newest = bf16[4,4,64,128]{3,2,1,0:T(8,128)(2,1)S(1)} all-gather(bf16[1,4,64,128]{3,2,1,0:T(8,128)(2,1)S(1)} %get-tuple-element.20), channel_id=1, replica_groups=mesh['space'=64,'lag'=4] {'lag'}, dimensions={0}, use_global_device_ids=true | all-gather | bytes 327680 | tf_op jit(solution)/shard_map/all_gather | solution.py:340
  8.2 0.0 copy-start.1
  8.2 0.8 %observe.1 = (bf16[80,1024]{1,0:T(8,128)(2,1)S(1)}, bf16[80,512]{1,0:T(8,128)(2,1)S(1)}, bf16[80,512]{1,0:T(8,128)(2,1)S(1)}) custom-call(s32[1]{0:T(128)} %bitcast.flag, bf16[4,4,64,128]{3,2,1,0:T(8,128)(2,1)S(1)} %all_gather.3.newest, f32[4,1024]{1,0:T(4,128)S(1)} %get-tuple-element.21.coef, s32[1,1024]{1,0:T(1,128)S(1)} %get-tuple-element.22.column, ...), custom_call_target="tpu_custom_call" | custom-call | tf_op jit(solution)/shard_map/observe/pallas_call | solution.py:266
  9.0 10.6 %collective-permute-start = (bf16[80,512]{1,0:T(8,128)(2,1)S(1)}, bf16[80,512]{1,0:T(8,128)(2,1)S(1)}, u32[]{:S(2)}, u32[]{:S(2)}) collective-permute-start(bf16[80,512]{1,0:T(8,128)(2,1)S(1)} %get-tuple-element.28), channel_id=1, source_target_pairs={{4,8},{8,4},{12,16},{16,12},{20,24},{24,20},{28,32},{32,28},{36,40... | collective-permute-start | bytes 245768 | tf_op jit(solution)/shard_map/ppermute | solution.py:343
  19.6 0.1 collective-permute-start.1
  19.7 0.0 copy-done.1
  19.7 0.0 copy-done.2
  19.7 0.0 copy-done.3
  19.7 0.4 %prepare.1 = (f32[512,128]{1,0:T(8,128)S(1)}, f32[8,128]{1,0:T(8,128)S(1)}, f32[64,128]{1,0:T(8,128)S(1)}, f32[64,128]{1,0:T(8,128)S(1)}, s32[64,128]{1,0:T(8,128)S(1)}) custom-call(s32[1]{0:T(128)} %bitcast.flag, s32[64,128]{1,0:T(8,128)S(1)} %copy-done.2, f32[64,128]{1,0:T(8,128)S(1)} %copy-done.3, bf16[2,4,64,128]{3,2,1,0:T(8,128)(2,1)S(1)} %copy-done.1), custom_call_target="tpu_custom_call" | custom-call | tf_op jit(solution)/shard_map/prepare/pallas_call | solution.py:286
  20.1 2.5 %collective-permute-done.first = bf16[80,512]{1,0:T(8,128)(2,1)S(1)} collective-permute-done((bf16[80,512]{1,0:T(8,128)(2,1)S(1)}, bf16[80,512]{1,0:T(8,128)(2,1)S(1)}, u32[]{:S(2)}, u32[]{:S(2)}) %collective-permute-start) | collective-permute-done | bytes 81952 | tf_op jit(solution)/shard_map/ppermute | solution.py:343
  22.5 1.6 %collective-permute-done.1.second = bf16[80,512]{1,0:T(8,128)(2,1)S(1)} collective-permute-done((bf16[80,512]{1,0:T(8,128)(2,1)S(1)}, bf16[80,512]{1,0:T(8,128)(2,1)S(1)}, u32[]{:S(2)}, u32[]{:S(2)}) %collective-permute-start.1) | collective-permute-done | bytes 81952 | tf_op jit(solution)/shard_map/ppermute | solution.py:342
  24.1 8.3 %solve.1 = bf16[2,4,64,128]{3,2,1,0:T(8,128)(2,1)} custom-call(bf16[80,1024]{1,0:T(8,128)(2,1)S(1)} %get-tuple-element.27.own, bf16[80,512]{1,0:T(8,128)(2,1)S(1)} %collective-permute-done.first, bf16[80,512]{1,0:T(8,128)(2,1)S(1)} %collective-permute-done.1.second, f32[512,128]{1,0:T(8,128)S(1)} %get-tuple-element.30.pd, ...), custom_call_target="tpu_custom_call" | custom-call | tf_op jit(solution)/shard_map/solve/pallas_call | solution.py:298
  (3 shorter events, 0.0 us)
Async XLA Ops:
  0.0 0.7 %copy-start.4 = (f32[4,1024]{1,0:T(4,128)S(1)}, f32[4,1024]{1,0:T(4,128)}, u32[]{:S(2)}) copy-start(f32[4,1024]{1,0:T(4,128)} %coef.1) | copy-start | bytes 49156
  0.0 0.7 %copy-start.8 = (s32[2,512]{1,0:T(2,128)S(1)}, s32[2,512]{1,0:T(2,128)}, u32[]{:S(2)}) copy-start(s32[2,512]{1,0:T(2,128)} %lists.1) | copy-start | bytes 12292
  0.0 0.7 %copy-start.7 = (f32[1024]{0:T(1024)S(1)}, f32[1024]{0:T(1024)}, u32[]{:S(2)}) copy-start(f32[1024]{0:T(1024)} %param.11) | copy-start | bytes 12292
  0.0 0.8 %copy-start.6 = (f32[1024]{0:T(1024)S(1)}, f32[1024]{0:T(1024)}, u32[]{:S(2)}) copy-start(f32[1024]{0:T(1024)} %param.10) | copy-start | bytes 12292
  0.0 0.8 %copy-start.5 = (s32[1024]{0:T(1024)S(1)}, s32[1024]{0:T(1024)}, u32[]{:S(2)}) copy-start(s32[1024]{0:T(1024)} %param.13) | copy-start | bytes 12292
  0.8 0.9 %copy-start = (bf16[2,4,64,128]{3,2,1,0:T(8,128)(2,1)S(1)}, bf16[2,4,64,128]{3,2,1,0:T(8,128)(2,1)}, u32[]{:S(2)}) copy-start(bf16[2,4,64,128]{3,2,1,0:T(8,128)(2,1)} %prior.3) | copy-start | bytes 393220
  8.2 11.5 %copy-start.1 = (bf16[2,4,64,128]{3,2,1,0:T(8,128)(2,1)S(1)}, bf16[2,4,64,128]{3,2,1,0:T(8,128)(2,1)}, u32[]{:S(2)}) copy-start(bf16[2,4,64,128]{3,2,1,0:T(8,128)(2,1)} %prior.3) | copy-start | bytes 393220
  8.2 11.5 %copy-start.2 = (s32[64,128]{1,0:T(8,128)S(1)}, s32[64,128]{1,0:T(8,128)}, u32[]{:S(2)}) copy-start(s32[64,128]{1,0:T(8,128)} %index.1) | copy-start | bytes 98308
  8.2 11.5 %copy-start.3 = (f32[64,128]{1,0:T(8,128)S(1)}, f32[64,128]{1,0:T(8,128)}, u32[]{:S(2)}) copy-start(f32[64,128]{1,0:T(8,128)} %local.1) | copy-start | bytes 98308
  9.0 13.6 %collective-permute-start = (bf16[80,512]{1,0:T(8,128)(2,1)S(1)}, bf16[80,512]{1,0:T(8,128)(2,1)S(1)}, u32[]{:S(2)}, u32[]{:S(2)}) collective-permute-start(bf16[80,512]{1,0:T(8,128)(2,1)S(1)} %get-tuple-element.28), channel_id=1, source_target_pairs={{4,8},{8,4},{12,16},{16,12},{20,24},{24,20},{28,32},{32,28},{36,40... | collective-permute-start | bytes 245768 | tf_op jit(solution)/shard_map/ppermute | solution.py:343
  19.6 4.5 %collective-permute-start.1 = (bf16[80,512]{1,0:T(8,128)(2,1)S(1)}, bf16[80,512]{1,0:T(8,128)(2,1)S(1)}, u32[]{:S(2)}, u32[]{:S(2)}) collective-permute-start(bf16[80,512]{1,0:T(8,128)(2,1)S(1)} %get-tuple-element.29), channel_id=1, source_target_pairs={{0,4},{4,0},{8,12},{12,8},{16,20},{20,16},{24,28},{28,24},{32,36},... | collective-permute-start | bytes 245768 | tf_op jit(solution)/shard_map/ppermute | solution.py:342

commit v6 on v5

--- a/solution.py
+++ b/solution.py
@@ -9,8 +9,8 @@
 K = 64
 HALF = 64
 ROWS = 80
-UA = 32
-UC = 32
+UA = 64
+UC = 64
 INTERPRET = False
 OBSERVE_BYTES = 12 << 20
 SOLVE_BYTES = 24 << 20
@@ -27,9 +27,9 @@
 
 
 def stage_kernel(
-    prior, coef, column, value, weight, lists, count,
-    newest_out, coef_out, column_out, value_out, weight_out, lists_out, count_out,
-    scalar, sems,
+    prior, coef, column, value, weight, lists,
+    newest_out, coef_out, column_out, value_out, weight_out, lists_out,
+    sems,
 ):
     lags = prior.shape[0]
     moves = (
@@ -39,14 +39,12 @@
         (value, value_out),
         (weight, weight_out),
         (lists, lists_out),
-        (count, scalar),
     )
     copies = [pltpu.make_async_copy(a, b, sems.at[n]) for n, (a, b) in enumerate(moves)]
     for copy in copies:
         copy.start()
     for copy in copies:
         copy.wait()
-    count_out[...] = jnp.full((1, 128), scalar[0], jnp.int32)
 
 
 def observe_kernel(flag, newest, coef, column, value, weight, lists, count, own, first, second):
@@ -105,9 +103,9 @@
 
     weights[...] = beside(local[...])
     places = beside(index[...].astype(F32)).astype(jnp.int32)
-    block = places >> 9
-    lows[...] = (places & 511).astype(F32)
-    codes[...] = jnp.where(block >= 2, block ^ flag[0], block)
+    block = places >> 8
+    lows[...] = (places & 255).astype(F32)
+    codes[...] = jnp.where(block >= 4, block ^ (2 * flag[0]), block)
 
     def rank(pair):
         lag, s = pair // spec, pair % spec
@@ -132,27 +130,39 @@
     left = lanes_of((HALF, 128)) < HALF
 
     row = lax.broadcasted_iota(jnp.int32, (HALF, 128), 0)
-    eye = jnp.where(row == (lanes_of((HALF, 128)) & (HALF - 1)), 1.0, 0.0)
+    eye = jnp.where(row == (lanes_of((HALF, 128)) & (HALF - 1)), K - 1.0, 0.0)
     leftb = lanes_of((HALF, 128)) < HALF
     ones = block_diagonal(jnp.ones((HALF, 128), F32), left).astype(BF16)
 
+    sources = [(own, b) for b in range(own.shape[1] // 256)]
+    sources += [(ref, b) for ref in (first, second) for b in range(halo // 256)]
+    blocks = len(sources)
+    views = [ref[:, b * 256 : (b + 1) * 256] for ref, b in sources]
+    infos = [view[HALF : HALF + 16].astype(F32) for view in views]
+    infos = [info[n : n + 1] for n in range(2) for info in infos]
     stacked = jnp.concatenate(
-        [own[:, 0:halo], own[:, halo:], first[...], second[...]], axis=0
+        [view[0:HALF] for view in views] + [jnp.concatenate(infos, axis=0).astype(BF16)], axis=0
     )
     counts = lax.broadcasted_iota(jnp.int32, (256, 256), 0).astype(F32).astype(BF16)
+    which = lax.broadcasted_iota(jnp.int32, (blocks, 256), 0)
+    high, none = jnp.ones((256, 256), BF16), jnp.zeros((256, 256), BF16)
 
     def pick(q):
         low = jnp.concatenate([lows[pl.ds(q, 1), :], lows[pl.ds(q + 1, 1), :]], axis=1)
         code = jnp.concatenate([codes[pl.ds(q, 1), :], codes[pl.ds(q + 1, 1), :]], axis=1)
-        hot = [
-            jnp.where(counts == (low - 256.0 * h).astype(BF16), 1.0, 0.0).astype(BF16)
-            for h in range(halo // 256)
+        found = dot(stacked, jnp.where(counts == low.astype(BF16), high, none))
+        total = found[0:HALF]
+        for b in range(1, blocks):
+            total = jnp.where(code == b, found[b * HALF : (b + 1) * HALF], total)
+        mine = which == code
+        info = [
+            jnp.sum(jnp.where(mine, found[at : at + blocks], 0.0), axis=0, keepdims=True)
+            for at in (blocks * HALF, blocks * HALF + blocks)
         ]
-        found = dot(stacked, jnp.concatenate(hot, axis=0))
-        total = found[0:ROWS]
-        for b in range(1, 4):
-            total = jnp.where(code == b, found[b * ROWS : (b + 1) * ROWS], total)
-        return total[:, 0:128], total[:, 128:]
+        return [
+            (total[:, at : at + 128], info[0][:, at : at + 128], info[1][:, at : at + 128])
+            for at in (0, 128)
+        ]
 
     @pl.loop(0, HALF // UA)
     def _(step):
@@ -161,11 +171,10 @@
         for q in qs[::2]:
             picked += pick(q)
         lefts, diagonals = [], []
-        for q, found in zip(qs, picked):
-            gathered = found[0:HALF]
-            scaled = weights[pl.ds(q, 1), :] * found[HALF : HALF + 1]
+        for q, (gathered, info0, info1) in zip(qs, picked):
+            scaled = weights[pl.ds(q, 1), :] * info0
             weighted = (gathered * scaled).astype(BF16)
-            pull = scaled * found[HALF + 1 : HALF + 2]
+            pull = scaled * info1
             pull_high = pull.astype(BF16).astype(F32)
             extra = jnp.concatenate([pull_high, pull - pull_high, jnp.zeros((14, 128), F32)], axis=0)
             lefts.append(jnp.concatenate([weighted, extra.astype(BF16)], axis=0))
@@ -175,7 +184,7 @@
             for l, d in zip(lefts, diagonals)
         ]
         for q, product in zip(qs, products):
-            full = eye + product[0:HALF] * (1.0 / (K - 1))
+            full = eye + product[0:HALF]
             matrix[q] = full
             squares[pl.ds(q, 1), :] = jnp.sum(full * full, axis=0, keepdims=True)
             drive = product[HALF : HALF + 1] + product[HALF + 1 : HALF + 2]
@@ -197,26 +206,23 @@
         first_powers = [matrix[q] * factors[pl.ds(q, 1), :] for q in qs]
         halves = [a.astype(BF16) for a in first_powers]
         second_powers = [dot(a, block_diagonal(a, leftb)) for a in halves]
-        mixes = [(-0.5625 * a + 0.0625 * b).astype(BF16) for a, b in zip(first_powers, second_powers)]
+        mixes = [(b - 9.0 * a).astype(BF16) for a, b in zip(first_powers, second_powers)]
         zs = [dot(c, block_diagonal(b.astype(BF16), leftb)) for c, b in zip(mixes, second_powers)]
-        zs = [
-            z + 2.25 * eye - 2.4375 * a + 1.6875 * b
-            for z, a, b in zip(zs, first_powers, second_powers)
-        ]
+        zs = [z + 27.0 * b - 39.0 * a for z, a, b in zip(zs, first_powers, second_powers)]
         eights = [pl.ds(pl.multiple_of(q * 8, 8), 8) for q in qs]
         sides = [jnp.concatenate([pd[at, :], tails[at, :]], axis=0).astype(BF16) for at in eights]
         products = [dot(p, block_diagonal(z.astype(BF16), leftb)) for p, z in zip(sides, zs)]
-        for q, product in zip(qs, products):
+        for at, side, product in zip(eights, sides, products):
+            product = product + 36.0 * side.astype(F32)
             mix = product[0:8]
             pulled = product[8:9] + product[9:10]
-            at = pl.ds(pl.multiple_of(q * 8, 8), 8)
             mixed[at, :] = mix
             shift[at, :] = mix * pulled
 
     shift[...] = half_sums(shift[...])
     one = factors[...]
-    root = jnp.sqrt(one)
-    one = one * (1.0 / (K - 1))
+    root = jnp.sqrt(one * (K - 1.0)) * (1.0 / 16.0)
+    one = one * (1.0 / 256.0)
 
     def final(pair):
         at = pl.ds(pair, HALF, stride=8)
@@ -242,22 +248,22 @@
     return pl.BlockSpec(memory_space=pltpu.HBM)
 
 
-def stage(prior, coef, column, value, weight, lists, count):
+def stage(*args):
+    prior, *rest = (pltpu.with_memory_space_constraint(x, pltpu.HBM) for x in args)
     shapes = [
         jax.ShapeDtypeStruct((1, *prior.shape[1:]), prior.dtype),
-        *(jax.ShapeDtypeStruct(x.shape, x.dtype) for x in (coef, column, value, weight, lists)),
-        jax.ShapeDtypeStruct((1, 128), jnp.int32),
+        *(jax.ShapeDtypeStruct(x.shape, x.dtype) for x in rest),
     ]
     return pl.pallas_call(
         stage_kernel,
         out_shape=shapes,
-        in_specs=[anywhere()] * 7,
-        out_specs=[vmem()] * 7,
-        scratch_shapes=[pltpu.SMEM((1,), jnp.int32), pltpu.SemaphoreType.DMA((7,))],
+        in_specs=[anywhere()] * 6,
+        out_specs=[vmem()] * 6,
+        scratch_shapes=[pltpu.SemaphoreType.DMA((6,))],
         compiler_params=pltpu.CompilerParams(vmem_limit_bytes=OBSERVE_BYTES),
         interpret=INTERPRET,
         name="stage",
-    )(prior, coef, column, value, weight, lists, count)
+    )(prior, *rest)
 
 
 def observe(flag, newest, coef, column, value, weight, lists, count):
@@ -335,10 +341,10 @@
     tiles = lax.axis_size("space")
     flag = (lax.axis_index("space") % 2)[None].astype(jnp.int32)
     newest, *staged = stage(
-        prior, obs_coef, obs_column[None], obs_value[None], obs_weight[None], halo_lists, obs_count
+        prior, obs_coef, obs_column[None], obs_value[None], obs_weight[None], halo_lists
     )
     newest = lax.all_gather(newest, "lag", axis=0, tiled=True)
-    own, first, second = observe(flag, newest, *staged)
+    own, first, second = observe(flag, newest, *staged, obs_count[None])
     second = lax.ppermute(second, "space", swaps(tiles, 0))
     first = lax.ppermute(first, "space", swaps(tiles, 1))
     ready = prepare(flag, neighbours, localization, prior)

time: 32.6 us -> 30.5 us (0.936)
  Pallas kernels: 10.1 us -> 9.04 us
  local copies, waits for them, and re-layouts: 0.93 us -> 0.01 us
    pallas_call x1, Pallas kernels: 8.29 us -> 7 us  [solve(): pl.pallas_call(solve_kernel, out_shape=jax.ShapeDtypeStruct(shape, BF16),...]
    unnamed x18 -> x6, local copies, waits for them, and re-layouts: 0.93 us -> 0.01 us
where the time goes in v6:
time: 30.5 us; the launch traced here: 30.3 us
  starting transfers between devices  10.7 us (35%)
  Pallas kernels  9.04 us (30%)
  blocking collectives  5.78 us (19%)
  waiting for transfers between devices  4.04 us (13%)
  between operations  0.72 us (2%)
    ppermute x1, starting transfers between devices, body(): first = lax.ppermute(first, 'space', swaps(tiles, 1))  10.6 us
    pallas_call x1, Pallas kernels, solve(): pl.pallas_call(solve_kernel, out_shape=jax.ShapeDtypeStruct(shape, BF16),...  7 us
    all_gather x1, blocking collectives, body(): newest = lax.all_gather(newest, 'lag', axis=0, tiled=True)  5.78 us
    ppermute x1, waiting for transfers between devices, body(): first = lax.ppermute(first, 'space', swaps(tiles, 1))  2.45 us
    ppermute x1, waiting for transfers between devices, body(): second = lax.ppermute(second, 'space', swaps(tiles, 0))  1.59 us
    pallas_call x1, Pallas kernels, stage(): pl.pallas_call(stage_kernel, out_shape=shapes, in_specs=[anywhere()] * 6,...  0.91 us
    pallas_call x1, Pallas kernels, observe(): pl.pallas_call(observe_kernel, out_shape=[jax.ShapeDtypeStruct(s, BF16) f...  0.78 us
  transfers between devices with their start and end apart: 2, of which 2 were waited for; matrix products, arithmetic and copies ran while one was open for 0% of the time, Pallas kernels for 1%

profile of v6, /device:TPU:24, one launch (start us, length us, event | category | flops | bytes accessed | tf_op | source)
XLA Modules:
  0.0 30.3 jit_solution(11922299216823470481)
XLA Ops:
  0.7 0.9 %stage.1 = (bf16[1,4,64,128]{3,2,1,0:T(8,128)(2,1)S(1)}, f32[4,1024]{1,0:T(4,128)S(1)}, s32[1,1024]{1,0:T(1,128)S(1)}, f32[1,1024]{1,0:T(1,128)S(1)}, f32[1,1024]{1,0:T(1,128)S(1)}, /*index=5*/s32[2,512]{1,0:T(2,128)S(1)}) custom-call(bf16[2,4,64,128]{3,2,1,0:T(8,128)(2,1)} %prior.3, f32[4,1024]{1,0:T(4,128)} %coef.1, s32[1,1024]{1,0:T(1,128)} %bitcast.6, ...), custom_call_target="tpu_custom_call" | custom-call | tf_op jit(solution)/shard_map/stage/pallas_call | solution.py:257
  1.6 5.8 %all_gather.3.newest = bf16[4,4,64,128]{3,2,1,0:T(8,128)(2,1)S(1)} all-gather(bf16[1,4,64,128]{3,2,1,0:T(8,128)(2,1)S(1)} %get-tuple-element.19), channel_id=1, replica_groups=mesh['space'=64,'lag'=4] {'lag'}, dimensions={0}, use_global_device_ids=true | all-gather | bytes 327680 | tf_op jit(solution)/shard_map/all_gather | solution.py:346
  7.3 0.0 copy-start
  7.3 0.0 copy-start.1
  7.3 0.0 copy-start.2
  7.4 0.8 %observe.1 = (bf16[80,1024]{1,0:T(8,128)(2,1)S(1)}, bf16[80,512]{1,0:T(8,128)(2,1)S(1)}, bf16[80,512]{1,0:T(8,128)(2,1)S(1)}) custom-call(s32[1]{0:T(128)} %bitcast.flag, bf16[4,4,64,128]{3,2,1,0:T(8,128)(2,1)S(1)} %all_gather.3.newest, f32[4,1024]{1,0:T(4,128)S(1)} %get-tuple-element.20.coef, s32[1,1024]{1,0:T(1,128)S(1)} %get-tuple-element.21.column, ...), custom_call_target="tpu_custom_call" | custom-call | tf_op jit(solution)/shard_map/observe/pallas_call | solution.py:272
  8.1 10.6 %collective-permute-start = (bf16[80,512]{1,0:T(8,128)(2,1)S(1)}, bf16[80,512]{1,0:T(8,128)(2,1)S(1)}, u32[]{:S(2)}, u32[]{:S(2)}) collective-permute-start(bf16[80,512]{1,0:T(8,128)(2,1)S(1)} %get-tuple-element.26), channel_id=1, source_target_pairs={{4,8},{8,4},{12,16},{16,12},{20,24},{24,20},{28,32},{32,28},{36,40... | collective-permute-start | bytes 245768 | tf_op jit(solution)/shard_map/ppermute | solution.py:349
  18.8 0.1 collective-permute-start.1
  18.9 0.0 copy-done
  18.9 0.0 copy-done.1
  18.9 0.0 copy-done.2
  18.9 0.4 %prepare.1 = (f32[512,128]{1,0:T(8,128)S(1)}, f32[8,128]{1,0:T(8,128)S(1)}, f32[64,128]{1,0:T(8,128)S(1)}, f32[64,128]{1,0:T(8,128)S(1)}, s32[64,128]{1,0:T(8,128)S(1)}) custom-call(s32[1]{0:T(128)} %bitcast.flag, s32[64,128]{1,0:T(8,128)S(1)} %copy-done.1, f32[64,128]{1,0:T(8,128)S(1)} %copy-done.2, bf16[2,4,64,128]{3,2,1,0:T(8,128)(2,1)S(1)} %copy-done), custom_call_target="tpu_custom_call" | custom-call | tf_op jit(solution)/shard_map/prepare/pallas_call | solution.py:292
  19.3 2.4 %collective-permute-done.first = bf16[80,512]{1,0:T(8,128)(2,1)S(1)} collective-permute-done((bf16[80,512]{1,0:T(8,128)(2,1)S(1)}, bf16[80,512]{1,0:T(8,128)(2,1)S(1)}, u32[]{:S(2)}, u32[]{:S(2)}) %collective-permute-start) | collective-permute-done | bytes 81952 | tf_op jit(solution)/shard_map/ppermute | solution.py:349
  21.7 1.6 %collective-permute-done.1.second = bf16[80,512]{1,0:T(8,128)(2,1)S(1)} collective-permute-done((bf16[80,512]{1,0:T(8,128)(2,1)S(1)}, bf16[80,512]{1,0:T(8,128)(2,1)S(1)}, u32[]{:S(2)}, u32[]{:S(2)}) %collective-permute-start.1) | collective-permute-done | bytes 81952 | tf_op jit(solution)/shard_map/ppermute | solution.py:348
  23.3 7.0 %solve.1 = bf16[2,4,64,128]{3,2,1,0:T(8,128)(2,1)} custom-call(bf16[80,1024]{1,0:T(8,128)(2,1)S(1)} %get-tuple-element.25.own, bf16[80,512]{1,0:T(8,128)(2,1)S(1)} %collective-permute-done.first, bf16[80,512]{1,0:T(8,128)(2,1)S(1)} %collective-permute-done.1.second, f32[512,128]{1,0:T(8,128)S(1)} %get-tuple-element.28.pd, ...), custom_call_target="tpu_custom_call" | custom-call | tf_op jit(solution)/shard_map/solve/pallas_call | solution.py:304
Async XLA Ops:
  7.3 11.5 %copy-start = (bf16[2,4,64,128]{3,2,1,0:T(8,128)(2,1)S(1)}, bf16[2,4,64,128]{3,2,1,0:T(8,128)(2,1)}, u32[]{:S(2)}) copy-start(bf16[2,4,64,128]{3,2,1,0:T(8,128)(2,1)} %prior.3) | copy-start | bytes 393220
  7.3 11.5 %copy-start.1 = (s32[64,128]{1,0:T(8,128)S(1)}, s32[64,128]{1,0:T(8,128)}, u32[]{:S(2)}) copy-start(s32[64,128]{1,0:T(8,128)} %index.1) | copy-start | bytes 98308
  7.3 11.5 %copy-start.2 = (f32[64,128]{1,0:T(8,128)S(1)}, f32[64,128]{1,0:T(8,128)}, u32[]{:S(2)}) copy-start(f32[64,128]{1,0:T(8,128)} %local.1) | copy-start | bytes 98308
  8.1 13.6 %collective-permute-start = (bf16[80,512]{1,0:T(8,128)(2,1)S(1)}, bf16[80,512]{1,0:T(8,128)(2,1)S(1)}, u32[]{:S(2)}, u32[]{:S(2)}) collective-permute-start(bf16[80,512]{1,0:T(8,128)(2,1)S(1)} %get-tuple-element.26), channel_id=1, source_target_pairs={{4,8},{8,4},{12,16},{16,12},{20,24},{24,20},{28,32},{32,28},{36,40... | collective-permute-start | bytes 245768 | tf_op jit(solution)/shard_map/ppermute | solution.py:349
  18.8 4.5 %collective-permute-start.1 = (bf16[80,512]{1,0:T(8,128)(2,1)S(1)}, bf16[80,512]{1,0:T(8,128)(2,1)S(1)}, u32[]{:S(2)}, u32[]{:S(2)}) collective-permute-start(bf16[80,512]{1,0:T(8,128)(2,1)S(1)} %get-tuple-element.27), channel_id=1, source_target_pairs={{0,4},{4,0},{8,12},{12,8},{16,20},{20,16},{24,28},{28,24},{32,36},... | collective-permute-start | bytes 245768 | tf_op jit(solution)/shard_map/ppermute | solution.py:348

commit v7 on v6

--- a/solution.py
+++ b/solution.py
@@ -9,6 +9,7 @@
 K = 64
 HALF = 64
 ROWS = 80
+UE = 64
 UA = 64
 UC = 64
 INTERPRET = False
@@ -120,58 +121,79 @@
         pd[pl.ds(pair + 1, HALF, stride=8), :] = packed(square, False)
 
 
-def solve_kernel(
-    own, first, second, pd, means, weights, lows, codes, out,
-    matrix, squares, factors, tails, mixed, shift,
-):
-    lags, spec = out.shape[0], out.shape[1]
-    count = lags * spec
-    halo = first.shape[1]
-    left = lanes_of((HALF, 128)) < HALF
-
-    row = lax.broadcasted_iota(jnp.int32, (HALF, 128), 0)
-    eye = jnp.where(row == (lanes_of((HALF, 128)) & (HALF - 1)), K - 1.0, 0.0)
-    leftb = lanes_of((HALF, 128)) < HALF
-    ones = block_diagonal(jnp.ones((HALF, 128), F32), left).astype(BF16)
-
-    sources = [(own, b) for b in range(own.shape[1] // 256)]
-    sources += [(ref, b) for ref in (first, second) for b in range(halo // 256)]
-    blocks = len(sources)
-    views = [ref[:, b * 256 : (b + 1) * 256] for ref, b in sources]
-    infos = [view[HALF : HALF + 16].astype(F32) for view in views]
+def gatherer(sources, codes_of, lows, codes):
+    blocks = 8
+    views = dict(zip(codes_of, (ref[:, b * 256 : (b + 1) * 256] for ref, b in sources)))
+    zero = jnp.zeros((16, 256), F32)
+    infos = [views[b][HALF : HALF + 16].astype(F32) if b in views else zero for b in range(blocks)]
     infos = [info[n : n + 1] for n in range(2) for info in infos]
     stacked = jnp.concatenate(
-        [view[0:HALF] for view in views] + [jnp.concatenate(infos, axis=0).astype(BF16)], axis=0
+        [views[b][0:HALF] for b in codes_of] + [jnp.concatenate(infos, axis=0).astype(BF16)], axis=0
     )
     counts = lax.broadcasted_iota(jnp.int32, (256, 256), 0).astype(F32).astype(BF16)
     which = lax.broadcasted_iota(jnp.int32, (blocks, 256), 0)
     high, none = jnp.ones((256, 256), BF16), jnp.zeros((256, 256), BF16)
-
-    def pick(q):
+    tail = len(codes_of) * HALF
+
+    def pick(q, total):
         low = jnp.concatenate([lows[pl.ds(q, 1), :], lows[pl.ds(q + 1, 1), :]], axis=1)
         code = jnp.concatenate([codes[pl.ds(q, 1), :], codes[pl.ds(q + 1, 1), :]], axis=1)
         found = dot(stacked, jnp.where(counts == low.astype(BF16), high, none))
-        total = found[0:HALF]
-        for b in range(1, blocks):
-            total = jnp.where(code == b, found[b * HALF : (b + 1) * HALF], total)
+        for n, b in enumerate(codes_of):
+            part = found[n * HALF : (n + 1) * HALF]
+            total = part if total is None else jnp.where(code == b, part, total)
         mine = which == code
         info = [
             jnp.sum(jnp.where(mine, found[at : at + blocks], 0.0), axis=0, keepdims=True)
-            for at in (blocks * HALF, blocks * HALF + blocks)
+            for at in (tail, tail + blocks)
         ]
         return [
             (total[:, at : at + 128], info[0][:, at : at + 128], info[1][:, at : at + 128])
             for at in (0, 128)
         ]
 
+    return pick
+
+
+def early_kernel(own, second, lows, codes, partial, info0_out, info1_out):
+    pick = gatherer(
+        [(own, b) for b in range(4)] + [(second, b) for b in range(2)],
+        (0, 1, 2, 3, 6, 7), lows, codes,
+    )
+
+    @pl.loop(0, HALF // UE)
+    def _(step):
+        for u in range(0, UE, 2):
+            q = step * UE + u
+            for n, (total, info0, info1) in enumerate(pick(q, None)):
+                partial[q + n] = total
+                info0_out[pl.ds(q + n, 1), :] = info0
+                info1_out[pl.ds(q + n, 1), :] = info1
+
+
+def solve_kernel(
+    first, partial, early0, early1, pd, means, weights, lows, codes, out,
+    matrix, squares, factors, tails, mixed, shift,
+):
+    lags, spec = out.shape[0], out.shape[1]
+    count = lags * spec
+    left = lanes_of((HALF, 128)) < HALF
+    row = lax.broadcasted_iota(jnp.int32, (HALF, 128), 0)
+    eye = jnp.where(row == (lanes_of((HALF, 128)) & (HALF - 1)), K - 1.0, 0.0)
+    leftb = lanes_of((HALF, 128)) < HALF
+    ones = block_diagonal(jnp.ones((HALF, 128), F32), left).astype(BF16)
+    pick = gatherer([(first, b) for b in range(2)], (4, 5), lows, codes)
+
     @pl.loop(0, HALF // UA)
     def _(step):
         qs = [step * UA + u for u in range(UA)]
         picked = []
         for q in qs[::2]:
-            picked += pick(q)
+            picked += pick(q, jnp.concatenate([partial[q], partial[q + 1]], axis=1))
         lefts, diagonals = [], []
         for q, (gathered, info0, info1) in zip(qs, picked):
+            info0 = info0 + early0[pl.ds(q, 1), :]
+            info1 = info1 + early1[pl.ds(q, 1), :]
             scaled = weights[pl.ds(q, 1), :] * info0
             weighted = (gathered * scaled).astype(BF16)
             pull = scaled * info1
@@ -300,11 +322,25 @@
     )(flag, index, local, prior)
 
 
+def early(own, second, lows, codes):
+    shapes = [(HALF, HALF, 128), (HALF, 128), (HALF, 128)]
+    return pl.pallas_call(
+        early_kernel,
+        out_shape=[jax.ShapeDtypeStruct(x, F32) for x in shapes],
+        in_specs=[vmem()] * 4,
+        out_specs=[vmem()] * 3,
+        compiler_params=pltpu.CompilerParams(vmem_limit_bytes=SOLVE_BYTES),
+        interpret=INTERPRET,
+        name="early",
+    )(own, second, lows, codes)
+
+
 def solve(own, first, second, pd, means, weights, lows, codes, shape):
+    partial = early(own, second, lows, codes)
     return pl.pallas_call(
         solve_kernel,
         out_shape=jax.ShapeDtypeStruct(shape, BF16),
-        in_specs=[vmem()] * 8,
+        in_specs=[vmem()] * 9,
         out_specs=vmem(),
         scratch_shapes=[
             pltpu.VMEM((HALF, HALF, 128), F32),
@@ -317,7 +353,7 @@
         compiler_params=pltpu.CompilerParams(vmem_limit_bytes=SOLVE_BYTES),
         interpret=INTERPRET,
         name="solve",
-    )(own, first, second, pd, means, weights, lows, codes)
+    )(first, *partial, pd, means, weights, lows, codes)
 
 
 def swaps(length, start):

time: 30.5 us -> 30.4 us (level)
  waiting for transfers between devices: 4.04 us -> 0.01 us
  local copies, waits for them, and re-layouts: 0.01 us -> 2.41 us
  starting transfers between devices: 10.7 us -> 11.5 us
  Pallas kernels: 9.04 us -> 9.61 us
    ppermute x1, waiting for transfers between devices: 2.45 us -> 0.01 us  [body(): first = lax.ppermute(first, 'space', swaps(tiles, 1))]
    unnamed x6, local copies, waits for them, and re-layouts: 0.01 us -> 2.41 us
    pallas_call x0 -> x1, Pallas kernels: none -> 1.91 us  [early(): pl.pallas_call(early_kernel, out_shape=[jax.ShapeDtypeStruct(x, F32) for...]
    ppermute x1, waiting for transfers between devices: 1.59 us -> 0.01 us  [body(): second = lax.ppermute(second, 'space', swaps(tiles, 0))]
    ppermute x1, starting transfers between devices: 0.09 us -> 1.58 us  [body(): second = lax.ppermute(second, 'space', swaps(tiles, 0))]
    pallas_call x1, Pallas kernels: 7 us -> 5.67 us  [solve(): pl.pallas_call(solve_kernel, out_shape=jax.ShapeDtypeStruct(shape, BF16),...]
    ppermute x1, starting transfers between devices: 10.6 us -> 9.96 us  [body(): first = lax.ppermute(first, 'space', swaps(tiles, 1))]
  transfers between devices with their start and end apart: 2 -> 2, of which waited for: 2 -> 0; matrix products, arithmetic and copies ran while one was open for 0% -> 0% of each run, Pallas kernels for 1% -> 8%
where the time goes in v7:
time: 30.4 us; the launch traced here: 30.1 us
  starting transfers between devices  11.5 us (38%)
  Pallas kernels  9.61 us (32%)
  blocking collectives  5.78 us (19%)
  local copies, waits for them, and re-layouts  2.41 us (8%)
  between operations  0.72 us (2%)
    ppermute x1, starting transfers between devices, body(): first = lax.ppermute(first, 'space', swaps(tiles, 1))  9.96 us
    all_gather x1, blocking collectives, body(): newest = lax.all_gather(newest, 'lag', axis=0, tiled=True)  5.78 us
    pallas_call x1, Pallas kernels, solve(): pl.pallas_call(solve_kernel, out_shape=jax.ShapeDtypeStruct(shape, BF16),...  5.67 us
    unnamed x6, local copies, waits for them, and re-layouts  2.41 us
    pallas_call x1, Pallas kernels, early(): pl.pallas_call(early_kernel, out_shape=[jax.ShapeDtypeStruct(x, F32) for...  1.91 us
    ppermute x1, starting transfers between devices, body(): second = lax.ppermute(second, 'space', swaps(tiles, 0))  1.58 us
    pallas_call x1, Pallas kernels, stage(): pl.pallas_call(stage_kernel, out_shape=shapes, in_specs=[anywhere()] * 6,...  0.91 us
    pallas_call x1, Pallas kernels, observe(): pl.pallas_call(observe_kernel, out_shape=[jax.ShapeDtypeStruct(s, BF16) f...  0.78 us
  transfers between devices with their start and end apart: 2, of which 0 were waited for; matrix products, arithmetic and copies ran while one was open for 0% of the time, Pallas kernels for 8%

profile of v7, /device:TPU:24, one launch (start us, length us, event | category | flops | bytes accessed | tf_op | source)
XLA Modules:
  0.0 30.1 jit_solution(8282339456564306401)
XLA Ops:
  0.7 0.9 %stage.1 = (bf16[1,4,64,128]{3,2,1,0:T(8,128)(2,1)S(1)}, f32[4,1024]{1,0:T(4,128)S(1)}, s32[1,1024]{1,0:T(1,128)S(1)}, f32[1,1024]{1,0:T(1,128)S(1)}, f32[1,1024]{1,0:T(1,128)S(1)}, /*index=5*/s32[2,512]{1,0:T(2,128)S(1)}) custom-call(bf16[2,4,64,128]{3,2,1,0:T(8,128)(2,1)} %prior.3, f32[4,1024]{1,0:T(4,128)} %coef.1, s32[1,1024]{1,0:T(1,128)} %bitcast.6, ...), custom_call_target="tpu_custom_call" | custom-call | tf_op jit(solution)/shard_map/stage/pallas_call | solution.py:279
  1.6 5.8 %all_gather.3.newest = bf16[4,4,64,128]{3,2,1,0:T(8,128)(2,1)S(1)} all-gather(bf16[1,4,64,128]{3,2,1,0:T(8,128)(2,1)S(1)} %get-tuple-element.22), channel_id=1, replica_groups=mesh['space'=64,'lag'=4] {'lag'}, dimensions={0}, use_global_device_ids=true | all-gather | bytes 327680 | tf_op jit(solution)/shard_map/all_gather | solution.py:382
  7.3 0.8 %observe.1 = (bf16[80,1024]{1,0:T(8,128)(2,1)S(1)}, bf16[80,512]{1,0:T(8,128)(2,1)S(1)}, bf16[80,512]{1,0:T(8,128)(2,1)S(1)}) custom-call(s32[1]{0:T(128)} %bitcast.flag, bf16[4,4,64,128]{3,2,1,0:T(8,128)(2,1)S(1)} %all_gather.3.newest, f32[4,1024]{1,0:T(4,128)S(1)} %get-tuple-element.23.coef, s32[1,1024]{1,0:T(1,128)S(1)} %get-tuple-element.24.column, ...), custom_call_target="tpu_custom_call" | custom-call | tf_op jit(solution)/shard_map/observe/pallas_call | solution.py:294
  8.1 1.6 %collective-permute-start.1 = (bf16[80,512]{1,0:T(8,128)(2,1)S(1)}, bf16[80,512]{1,0:T(8,128)(2,1)S(1)}, u32[]{:S(2)}, u32[]{:S(2)}) collective-permute-start(bf16[80,512]{1,0:T(8,128)(2,1)S(1)} %get-tuple-element.30), channel_id=1, source_target_pairs={{0,4},{4,0},{8,12},{12,8},{16,20},{20,16},{24,28},{28,24},{32,36},... | collective-permute-start | bytes 245768 | tf_op jit(solution)/shard_map/ppermute | solution.py:384
  9.7 10.0 %collective-permute-start = (bf16[80,512]{1,0:T(8,128)(2,1)S(1)}, bf16[80,512]{1,0:T(8,128)(2,1)S(1)}, u32[]{:S(2)}, u32[]{:S(2)}) collective-permute-start(bf16[80,512]{1,0:T(8,128)(2,1)S(1)} %get-tuple-element.28), channel_id=1, source_target_pairs={{4,8},{8,4},{12,16},{16,12},{20,24},{24,20},{28,32},{32,28},{36,40... | collective-permute-start | bytes 245768 | tf_op jit(solution)/shard_map/ppermute | solution.py:385
  19.7 0.0 copy-start
  19.7 0.9 %copy-done = bf16[2,4,64,128]{3,2,1,0:T(8,128)(2,1)S(1)} copy-done((bf16[2,4,64,128]{3,2,1,0:T(8,128)(2,1)S(1)}, bf16[2,4,64,128]{3,2,1,0:T(8,128)(2,1)}, u32[]{:S(2)}) %copy-start) | copy-done | bytes 131096
  20.6 0.0 copy-start.1
  20.6 0.8 %copy-done.1 = s32[64,128]{1,0:T(8,128)S(1)} copy-done((s32[64,128]{1,0:T(8,128)S(1)}, s32[64,128]{1,0:T(8,128)}, u32[]{:S(2)}) %copy-start.1) | copy-done | bytes 32792
  21.3 0.0 copy-start.2
  21.3 0.8 %copy-done.2 = f32[64,128]{1,0:T(8,128)S(1)} copy-done((f32[64,128]{1,0:T(8,128)S(1)}, f32[64,128]{1,0:T(8,128)}, u32[]{:S(2)}) %copy-start.2) | copy-done | bytes 32792
  22.1 0.3 %prepare.1 = (f32[512,128]{1,0:T(8,128)S(1)}, f32[8,128]{1,0:T(8,128)S(1)}, f32[64,128]{1,0:T(8,128)S(1)}, f32[64,128]{1,0:T(8,128)S(1)}, s32[64,128]{1,0:T(8,128)S(1)}) custom-call(s32[1]{0:T(128)} %bitcast.flag, s32[64,128]{1,0:T(8,128)S(1)} %copy-done.1, f32[64,128]{1,0:T(8,128)S(1)} %copy-done.2, bf16[2,4,64,128]{3,2,1,0:T(8,128)(2,1)S(1)} %copy-done), custom_call_target="tpu_custom_call" | custom-call | tf_op jit(solution)/shard_map/prepare/pallas_call | solution.py:314
  22.5 0.0 collective-permute-done.1.second
  22.5 1.9 %early.1 = (f32[64,64,128]{2,1,0:T(8,128)S(1)}, f32[64,128]{1,0:T(8,128)S(1)}, f32[64,128]{1,0:T(8,128)S(1)}) custom-call(bf16[80,1024]{1,0:T(8,128)(2,1)S(1)} %get-tuple-element.29.own, bf16[80,512]{1,0:T(8,128)(2,1)S(1)} %collective-permute-done.1.second, f32[64,128]{1,0:T(8,128)S(1)} %get-tuple-element.31.lows, s32[64,128]{1,0:T(8,128)S(1)} %get-tuple-element.32.codes), custom_call_target="tpu_custom_call" | custom-call | tf_op jit(solution)/shard_map/early/pallas_call | solution.py:327
  24.4 0.0 collective-permute-done.first
  24.4 5.7 %solve.1 = bf16[2,4,64,128]{3,2,1,0:T(8,128)(2,1)} custom-call(bf16[80,512]{1,0:T(8,128)(2,1)S(1)} %collective-permute-done.first, f32[64,64,128]{2,1,0:T(8,128)S(1)} %get-tuple-element.33.partial, f32[64,128]{1,0:T(8,128)S(1)} %get-tuple-element.34.early0, f32[64,128]{1,0:T(8,128)S(1)} %get-tuple-element.35.early1, f32[512,128]{1,0:T(8,128)S(1)} %get-tuple-element.36.pd, ...), custom_call_target="tpu_custom_call" | custom-call | tf_op jit(solution)/shard_map/solve/pallas_call | solution.py:340
Async XLA Ops:
  8.1 14.3 %collective-permute-start.1 = (bf16[80,512]{1,0:T(8,128)(2,1)S(1)}, bf16[80,512]{1,0:T(8,128)(2,1)S(1)}, u32[]{:S(2)}, u32[]{:S(2)}) collective-permute-start(bf16[80,512]{1,0:T(8,128)(2,1)S(1)} %get-tuple-element.30), channel_id=1, source_target_pairs={{0,4},{4,0},{8,12},{12,8},{16,20},{20,16},{24,28},{28,24},{32,36},... | collective-permute-start | bytes 245768 | tf_op jit(solution)/shard_map/ppermute | solution.py:384
  9.7 14.7 %collective-permute-start = (bf16[80,512]{1,0:T(8,128)(2,1)S(1)}, bf16[80,512]{1,0:T(8,128)(2,1)S(1)}, u32[]{:S(2)}, u32[]{:S(2)}) collective-permute-start(bf16[80,512]{1,0:T(8,128)(2,1)S(1)} %get-tuple-element.28), channel_id=1, source_target_pairs={{4,8},{8,4},{12,16},{16,12},{20,24},{24,20},{28,32},{32,28},{36,40... | collective-permute-start | bytes 245768 | tf_op jit(solution)/shard_map/ppermute | solution.py:385
  19.7 0.9 %copy-start = (bf16[2,4,64,128]{3,2,1,0:T(8,128)(2,1)S(1)}, bf16[2,4,64,128]{3,2,1,0:T(8,128)(2,1)}, u32[]{:S(2)}) copy-start(bf16[2,4,64,128]{3,2,1,0:T(8,128)(2,1)} %prior.3) | copy-start | bytes 393220
  20.6 0.8 %copy-start.1 = (s32[64,128]{1,0:T(8,128)S(1)}, s32[64,128]{1,0:T(8,128)}, u32[]{:S(2)}) copy-start(s32[64,128]{1,0:T(8,128)} %index.1) | copy-start | bytes 98308
  21.3 0.8 %copy-start.2 = (f32[64,128]{1,0:T(8,128)S(1)}, f32[64,128]{1,0:T(8,128)}, u32[]{:S(2)}) copy-start(f32[64,128]{1,0:T(8,128)} %local.1) | copy-start | bytes 98308

commit v8 on v7

--- a/solution.py
+++ b/solution.py
@@ -48,7 +48,14 @@
         copy.wait()
 
 
-def observe_kernel(flag, newest, coef, column, value, weight, lists, count, own, first, second):
+def observe_kernel(
+    flag, newest, coef, column, value, weight, lists, count, prior, index, local,
+    own, first, second, prior_out, index_out, local_out, sems,
+):
+    moves = ((prior, prior_out), (index, index_out), (local, local_out))
+    copies = [pltpu.make_async_copy(a, b, sems.at[n]) for n, (a, b) in enumerate(moves)]
+    for copy in copies:
+        copy.start()
     slots = column.shape[1]
     lags, spec = newest.shape[0], newest.shape[1]
     halo = lists.shape[1]
@@ -80,6 +87,8 @@
         for b in range(1, blocks):
             total = jnp.where(high == b, found[b * ROWS : (b + 1) * ROWS], total)
         out[...] = total.astype(BF16)
+    for copy in copies:
+        copy.wait()
 
 
 def packed(square, lower):
@@ -288,18 +297,21 @@
     )(prior, *rest)
 
 
-def observe(flag, newest, coef, column, value, weight, lists, count):
+def observe(flag, newest, coef, column, value, weight, lists, count, *later):
     slots, halo = column.shape[1], lists.shape[1]
     shapes = [(ROWS, slots), (ROWS, halo), (ROWS, halo)]
+    later = [pltpu.with_memory_space_constraint(x, pltpu.HBM) for x in later]
     return pl.pallas_call(
         observe_kernel,
-        out_shape=[jax.ShapeDtypeStruct(s, BF16) for s in shapes],
-        in_specs=[smem()] + [vmem()] * 7,
-        out_specs=[vmem()] * 3,
+        out_shape=[jax.ShapeDtypeStruct(s, BF16) for s in shapes]
+        + [jax.ShapeDtypeStruct(x.shape, x.dtype) for x in later],
+        in_specs=[smem()] + [vmem()] * 7 + [anywhere()] * 3,
+        out_specs=[vmem()] * 6,
+        scratch_shapes=[pltpu.SemaphoreType.DMA((3,))],
         compiler_params=pltpu.CompilerParams(vmem_limit_bytes=OBSERVE_BYTES),
         interpret=INTERPRET,
         name="observe",
-    )(flag, newest, coef, column, value, weight, lists, count)
+    )(flag, newest, coef, column, value, weight, lists, count, *later)
 
 
 def prepare(flag, index, local, prior):
@@ -380,10 +392,12 @@
         prior, obs_coef, obs_column[None], obs_value[None], obs_weight[None], halo_lists
     )
     newest = lax.all_gather(newest, "lag", axis=0, tiled=True)
-    own, first, second = observe(flag, newest, *staged, obs_count[None])
+    own, first, second, prior, index, local = observe(
+        flag, newest, *staged, obs_count[None], prior, neighbours, localization
+    )
     second = lax.ppermute(second, "space", swaps(tiles, 0))
     first = lax.ppermute(first, "space", swaps(tiles, 1))
-    ready = prepare(flag, neighbours, localization, prior)
+    ready = prepare(flag, index, local, prior)
     return solve(own, first, second, *ready, prior.shape)
 
 

time: 30.4 us -> 28.5 us (0.938)
  local copies, waits for them, and re-layouts: 2.41 us -> 0 us
  waiting for transfers between devices: 0.01 us -> 0.37 us
  Pallas kernels: 9.61 us -> 9.93 us
    unnamed x6 -> x0, local copies, waits for them, and re-layouts: 2.41 us -> none
    ppermute x1, waiting for transfers between devices: 0.01 us -> 0.36 us  [body(): first = lax.ppermute(first, 'space', swaps(tiles, 1))]
    pallas_call x1, Pallas kernels: 0.78 us -> 1.09 us  [observe(): pl.pallas_call(observe_kernel, out_shape=[jax.ShapeDtypeStruct(s, BF16) f...]
  transfers between devices with their start and end apart: 2 -> 2, of which waited for: 0 -> 1; matrix products, arithmetic and copies ran while one was open for 0% -> 0% of each run, Pallas kernels for 8% -> 8%
where the time goes in v8:
time: 28.5 us; the launch traced here: 28.3 us
  starting transfers between devices  11.5 us (40%)
  Pallas kernels  9.93 us (35%)
  blocking collectives  5.78 us (20%)
  between operations  0.7 us (2%)
  waiting for transfers between devices  0.37 us (1%)
    ppermute x1, starting transfers between devices, body(): first = lax.ppermute(first, 'space', swaps(tiles, 1))  9.95 us
    all_gather x1, blocking collectives, body(): newest = lax.all_gather(newest, 'lag', axis=0, tiled=True)  5.78 us
    pallas_call x1, Pallas kernels, solve(): pl.pallas_call(solve_kernel, out_shape=jax.ShapeDtypeStruct(shape, BF16),...  5.66 us
    pallas_call x1, Pallas kernels, early(): pl.pallas_call(early_kernel, out_shape=[jax.ShapeDtypeStruct(x, F32) for...  1.91 us
    ppermute x1, starting transfers between devices, body(): second = lax.ppermute(second, 'space', swaps(tiles, 0))  1.58 us
    pallas_call x1, Pallas kernels, observe(): pl.pallas_call(observe_kernel, out_shape=[jax.ShapeDtypeStruct(s, BF16) f...  1.09 us
    pallas_call x1, Pallas kernels, stage(): pl.pallas_call(stage_kernel, out_shape=shapes, in_specs=[anywhere()] * 6,...  0.91 us
  transfers between devices with their start and end apart: 2, of which 1 were waited for; matrix products, arithmetic and copies ran while one was open for 0% of the time, Pallas kernels for 8%

profile of v8, /device:TPU:24, one launch (start us, length us, event | category | flops | bytes accessed | tf_op | source)
XLA Modules:
  0.0 28.3 jit_solution(5275683705790490735)
XLA Ops:
  0.7 0.9 %stage.1 = (bf16[1,4,64,128]{3,2,1,0:T(8,128)(2,1)S(1)}, f32[4,1024]{1,0:T(4,128)S(1)}, s32[1,1024]{1,0:T(1,128)S(1)}, f32[1,1024]{1,0:T(1,128)S(1)}, f32[1,1024]{1,0:T(1,128)S(1)}, /*index=5*/s32[2,512]{1,0:T(2,128)S(1)}) custom-call(bf16[2,4,64,128]{3,2,1,0:T(8,128)(2,1)} %prior.3, f32[4,1024]{1,0:T(4,128)} %coef.1, s32[1,1024]{1,0:T(1,128)} %bitcast.6, ...), custom_call_target="tpu_custom_call" | custom-call | tf_op jit(solution)/shard_map/stage/pallas_call | solution.py:288
  1.6 5.8 %all_gather.3.newest = bf16[4,4,64,128]{3,2,1,0:T(8,128)(2,1)S(1)} all-gather(bf16[1,4,64,128]{3,2,1,0:T(8,128)(2,1)S(1)} %get-tuple-element.25), channel_id=1, replica_groups=mesh['space'=64,'lag'=4] {'lag'}, dimensions={0}, use_global_device_ids=true | all-gather | bytes 327680 | tf_op jit(solution)/shard_map/all_gather | solution.py:394
  7.3 1.1 %observe.1 = (bf16[80,1024]{1,0:T(8,128)(2,1)S(1)}, bf16[80,512]{1,0:T(8,128)(2,1)S(1)}, bf16[80,512]{1,0:T(8,128)(2,1)S(1)}, bf16[2,4,64,128]{3,2,1,0:T(8,128)(...) custom-call(s32[1]{0:T(128)} %bitcast.flag, bf16[4,4,64,128]{3,2,1,0:T(8,128)(2,1)S(1)} %all_gather.3.newest, ...), custom_call_target="tpu_custom_call" | custom-call | tf_op jit(solution)/shard_map/observe/pallas_call | solution.py:304
  8.4 1.6 %collective-permute-start.1 = (bf16[80,512]{1,0:T(8,128)(2,1)S(1)}, bf16[80,512]{1,0:T(8,128)(2,1)S(1)}, u32[]{:S(2)}, u32[]{:S(2)}) collective-permute-start(bf16[80,512]{1,0:T(8,128)(2,1)S(1)} %get-tuple-element.33), channel_id=1, source_target_pairs={{0,4},{4,0},{8,12},{12,8},{16,20},{20,16},{24,28},{28,24},{32,36},... | collective-permute-start | bytes 245768 | tf_op jit(solution)/shard_map/ppermute | solution.py:398
  10.0 10.0 %collective-permute-start = (bf16[80,512]{1,0:T(8,128)(2,1)S(1)}, bf16[80,512]{1,0:T(8,128)(2,1)S(1)}, u32[]{:S(2)}, u32[]{:S(2)}) collective-permute-start(bf16[80,512]{1,0:T(8,128)(2,1)S(1)} %get-tuple-element.31), channel_id=1, source_target_pairs={{4,8},{8,4},{12,16},{16,12},{20,24},{24,20},{28,32},{32,28},{36,40... | collective-permute-start | bytes 245768 | tf_op jit(solution)/shard_map/ppermute | solution.py:399
  20.0 0.4 %prepare.1 = (f32[512,128]{1,0:T(8,128)S(1)}, f32[8,128]{1,0:T(8,128)S(1)}, f32[64,128]{1,0:T(8,128)S(1)}, f32[64,128]{1,0:T(8,128)S(1)}, s32[64,128]{1,0:T(8,128)S(1)}) custom-call(s32[1]{0:T(128)} %bitcast.flag, s32[64,128]{1,0:T(8,128)S(1)} %get-tuple-element.34.index, f32[64,128]{1,0:T(8,128)S(1)} %get-tuple-element.35.local, ...), custom_call_target="tpu_custom_call" | custom-call | tf_op jit(solution)/shard_map/prepare/pallas_call | solution.py:326
  20.4 0.0 collective-permute-done.1.second
  20.4 1.9 %early.1 = (f32[64,64,128]{2,1,0:T(8,128)S(1)}, f32[64,128]{1,0:T(8,128)S(1)}, f32[64,128]{1,0:T(8,128)S(1)}) custom-call(bf16[80,1024]{1,0:T(8,128)(2,1)S(1)} %get-tuple-element.32.own, bf16[80,512]{1,0:T(8,128)(2,1)S(1)} %collective-permute-done.1.second, f32[64,128]{1,0:T(8,128)S(1)} %get-tuple-element.37.lows, s32[64,128]{1,0:T(8,128)S(1)} %get-tuple-element.38.codes), custom_call_target="tpu_custom_call" | custom-call | tf_op jit(solution)/shard_map/early/pallas_call | solution.py:339
  22.3 0.4 %collective-permute-done.first = bf16[80,512]{1,0:T(8,128)(2,1)S(1)} collective-permute-done((bf16[80,512]{1,0:T(8,128)(2,1)S(1)}, bf16[80,512]{1,0:T(8,128)(2,1)S(1)}, u32[]{:S(2)}, u32[]{:S(2)}) %collective-permute-start) | collective-permute-done | bytes 81952 | tf_op jit(solution)/shard_map/ppermute | solution.py:399
  22.6 5.7 %solve.1 = bf16[2,4,64,128]{3,2,1,0:T(8,128)(2,1)} custom-call(bf16[80,512]{1,0:T(8,128)(2,1)S(1)} %collective-permute-done.first, f32[64,64,128]{2,1,0:T(8,128)S(1)} %get-tuple-element.39.partial, f32[64,128]{1,0:T(8,128)S(1)} %get-tuple-element.40.early0, f32[64,128]{1,0:T(8,128)S(1)} %get-tuple-element.41.early1, f32[512,128]{1,0:T(8,128)S(1)} %get-tuple-element.42.pd, ...), custom_call_target="tpu_custom_call" | custom-call | tf_op jit(solution)/shard_map/solve/pallas_call | solution.py:352
Async XLA Ops:
  8.4 11.9 %collective-permute-start.1 = (bf16[80,512]{1,0:T(8,128)(2,1)S(1)}, bf16[80,512]{1,0:T(8,128)(2,1)S(1)}, u32[]{:S(2)}, u32[]{:S(2)}) collective-permute-start(bf16[80,512]{1,0:T(8,128)(2,1)S(1)} %get-tuple-element.33), channel_id=1, source_target_pairs={{0,4},{4,0},{8,12},{12,8},{16,20},{20,16},{24,28},{28,24},{32,36},... | collective-permute-start | bytes 245768 | tf_op jit(solution)/shard_map/ppermute | solution.py:398
  10.0 12.6 %collective-permute-start = (bf16[80,512]{1,0:T(8,128)(2,1)S(1)}, bf16[80,512]{1,0:T(8,128)(2,1)S(1)}, u32[]{:S(2)}, u32[]{:S(2)}) collective-permute-start(bf16[80,512]{1,0:T(8,128)(2,1)S(1)} %get-tuple-element.31), channel_id=1, source_target_pairs={{4,8},{8,4},{12,16},{16,12},{20,24},{24,20},{28,32},{32,28},{36,40... | collective-permute-start | bytes 245768 | tf_op jit(solution)/shard_map/ppermute | solution.py:399

commit v9 on v8

--- a/solution.py
+++ b/solution.py
@@ -128,6 +128,13 @@
         square = jnp.concatenate([rank(pair), rank(pair + 1)], axis=0).T
         pd[pl.ds(pair, HALF, stride=8), :] = packed(square, True)
         pd[pl.ds(pair + 1, HALF, stride=8), :] = packed(square, False)
+
+
+def apart(rows, pair):
+    left = lanes_of((16, 128)) < HALF
+    lhs = jnp.concatenate([rows, pltpu.roll(rows, HALF, 1)], axis=0)[:, 0:HALF].astype(BF16)
+    product = dot(lhs, pair)
+    return jnp.where(left, product[0:16], product[16:])
 
 
 def gatherer(sources, codes_of, lows, codes):
@@ -234,17 +241,20 @@
     @pl.loop(0, HALF // UC)
     def _(step):
         qs = [step * UC + u for u in range(UC)]
-        first_powers = [matrix[q] * factors[pl.ds(q, 1), :] for q in qs]
-        halves = [a.astype(BF16) for a in first_powers]
-        second_powers = [dot(a, block_diagonal(a, leftb)) for a in halves]
-        mixes = [(b - 9.0 * a).astype(BF16) for a, b in zip(first_powers, second_powers)]
-        zs = [dot(c, block_diagonal(b.astype(BF16), leftb)) for c, b in zip(mixes, second_powers)]
-        zs = [z + 27.0 * b - 39.0 * a for z, a, b in zip(zs, first_powers, second_powers)]
         eights = [pl.ds(pl.multiple_of(q * 8, 8), 8) for q in qs]
-        sides = [jnp.concatenate([pd[at, :], tails[at, :]], axis=0).astype(BF16) for at in eights]
-        products = [dot(p, block_diagonal(z.astype(BF16), leftb)) for p, z in zip(sides, zs)]
-        for at, side, product in zip(eights, sides, products):
-            product = product + 36.0 * side.astype(F32)
+        sides = [jnp.concatenate([pd[at, :], tails[at, :]], axis=0) for at in eights]
+        halves = [(matrix[q] * factors[pl.ds(q, 1), :]).astype(BF16) for q in qs]
+        low = [side.astype(BF16) for side in sides]
+        once = [
+            dot(jnp.concatenate([a, p], axis=0), block_diagonal(a, leftb))
+            for a, p in zip(halves, low)
+        ]
+        seconds = [o[0:HALF].astype(BF16) for o in once]
+        once = [o[HALF:] for o in once]
+        twice = [apart(p, b) for p, b in zip(sides, seconds)]
+        rest = [apart(t - 9.0 * o, b) for t, o, b in zip(twice, once, seconds)]
+        for at, side, o, t, r in zip(eights, sides, once, twice, rest):
+            product = 36.0 * side - 39.0 * o + 27.0 * t + r
             mix = product[0:8]
             pulled = product[8:9] + product[9:10]
             mixed[at, :] = mix

time: 28.5 us -> 28 us (0.982)
  Pallas kernels: 9.93 us -> 9.48 us
    pallas_call x1, Pallas kernels: 5.66 us -> 5.21 us  [solve(): pl.pallas_call(solve_kernel, out_shape=jax.ShapeDtypeStruct(shape, BF16),...]
where the time goes in v9:
time: 28 us; the launch traced here: 27.9 us
  starting transfers between devices  11.5 us (41%)
  Pallas kernels  9.48 us (34%)
  blocking collectives  5.78 us (21%)
  between operations  0.7 us (2%)
  waiting for transfers between devices  0.37 us (1%)
    ppermute x1, starting transfers between devices, body(): first = lax.ppermute(first, 'space', swaps(tiles, 1))  9.95 us
    all_gather x1, blocking collectives, body(): newest = lax.all_gather(newest, 'lag', axis=0, tiled=True)  5.78 us
    pallas_call x1, Pallas kernels, solve(): pl.pallas_call(solve_kernel, out_shape=jax.ShapeDtypeStruct(shape, BF16),...  5.21 us
    pallas_call x1, Pallas kernels, early(): pl.pallas_call(early_kernel, out_shape=[jax.ShapeDtypeStruct(x, F32) for...  1.91 us
    ppermute x1, starting transfers between devices, body(): second = lax.ppermute(second, 'space', swaps(tiles, 0))  1.58 us
    pallas_call x1, Pallas kernels, observe(): pl.pallas_call(observe_kernel, out_shape=[jax.ShapeDtypeStruct(s, BF16) f...  1.09 us
    pallas_call x1, Pallas kernels, stage(): pl.pallas_call(stage_kernel, out_shape=shapes, in_specs=[anywhere()] * 6,...  0.91 us
  transfers between devices with their start and end apart: 2, of which 1 were waited for; matrix products, arithmetic and copies ran while one was open for 0% of the time, Pallas kernels for 8%

profile of v9, /device:TPU:24, one launch (start us, length us, event | category | flops | bytes accessed | tf_op | source)
XLA Modules:
  0.0 27.9 jit_solution(5073716219097372736)
XLA Ops:
  0.7 0.9 %stage.1 = (bf16[1,4,64,128]{3,2,1,0:T(8,128)(2,1)S(1)}, f32[4,1024]{1,0:T(4,128)S(1)}, s32[1,1024]{1,0:T(1,128)S(1)}, f32[1,1024]{1,0:T(1,128)S(1)}, f32[1,1024]{1,0:T(1,128)S(1)}, /*index=5*/s32[2,512]{1,0:T(2,128)S(1)}) custom-call(bf16[2,4,64,128]{3,2,1,0:T(8,128)(2,1)} %prior.3, f32[4,1024]{1,0:T(4,128)} %coef.1, s32[1,1024]{1,0:T(1,128)} %bitcast.6, ...), custom_call_target="tpu_custom_call" | custom-call | tf_op jit(solution)/shard_map/stage/pallas_call | solution.py:298
  1.6 5.8 %all_gather.3.newest = bf16[4,4,64,128]{3,2,1,0:T(8,128)(2,1)S(1)} all-gather(bf16[1,4,64,128]{3,2,1,0:T(8,128)(2,1)S(1)} %get-tuple-element.25), channel_id=1, replica_groups=mesh['space'=64,'lag'=4] {'lag'}, dimensions={0}, use_global_device_ids=true | all-gather | bytes 327680 | tf_op jit(solution)/shard_map/all_gather | solution.py:404
  7.3 1.1 %observe.1 = (bf16[80,1024]{1,0:T(8,128)(2,1)S(1)}, bf16[80,512]{1,0:T(8,128)(2,1)S(1)}, bf16[80,512]{1,0:T(8,128)(2,1)S(1)}, bf16[2,4,64,128]{3,2,1,0:T(8,128)(...) custom-call(s32[1]{0:T(128)} %bitcast.flag, bf16[4,4,64,128]{3,2,1,0:T(8,128)(2,1)S(1)} %all_gather.3.newest, ...), custom_call_target="tpu_custom_call" | custom-call | tf_op jit(solution)/shard_map/observe/pallas_call | solution.py:314
  8.4 1.6 %collective-permute-start.1 = (bf16[80,512]{1,0:T(8,128)(2,1)S(1)}, bf16[80,512]{1,0:T(8,128)(2,1)S(1)}, u32[]{:S(2)}, u32[]{:S(2)}) collective-permute-start(bf16[80,512]{1,0:T(8,128)(2,1)S(1)} %get-tuple-element.33), channel_id=1, source_target_pairs={{0,4},{4,0},{8,12},{12,8},{16,20},{20,16},{24,28},{28,24},{32,36},... | collective-permute-start | bytes 245768 | tf_op jit(solution)/shard_map/ppermute | solution.py:408
  10.0 10.0 %collective-permute-start = (bf16[80,512]{1,0:T(8,128)(2,1)S(1)}, bf16[80,512]{1,0:T(8,128)(2,1)S(1)}, u32[]{:S(2)}, u32[]{:S(2)}) collective-permute-start(bf16[80,512]{1,0:T(8,128)(2,1)S(1)} %get-tuple-element.31), channel_id=1, source_target_pairs={{4,8},{8,4},{12,16},{16,12},{20,24},{24,20},{28,32},{32,28},{36,40... | collective-permute-start | bytes 245768 | tf_op jit(solution)/shard_map/ppermute | solution.py:409
  20.0 0.4 %prepare.1 = (f32[512,128]{1,0:T(8,128)S(1)}, f32[8,128]{1,0:T(8,128)S(1)}, f32[64,128]{1,0:T(8,128)S(1)}, f32[64,128]{1,0:T(8,128)S(1)}, s32[64,128]{1,0:T(8,128)S(1)}) custom-call(s32[1]{0:T(128)} %bitcast.flag, s32[64,128]{1,0:T(8,128)S(1)} %get-tuple-element.34.index, f32[64,128]{1,0:T(8,128)S(1)} %get-tuple-element.35.local, ...), custom_call_target="tpu_custom_call" | custom-call | tf_op jit(solution)/shard_map/prepare/pallas_call | solution.py:336
  20.4 0.0 collective-permute-done.1.second
  20.4 1.9 %early.1 = (f32[64,64,128]{2,1,0:T(8,128)S(1)}, f32[64,128]{1,0:T(8,128)S(1)}, f32[64,128]{1,0:T(8,128)S(1)}) custom-call(bf16[80,1024]{1,0:T(8,128)(2,1)S(1)} %get-tuple-element.32.own, bf16[80,512]{1,0:T(8,128)(2,1)S(1)} %collective-permute-done.1.second, f32[64,128]{1,0:T(8,128)S(1)} %get-tuple-element.37.lows, s32[64,128]{1,0:T(8,128)S(1)} %get-tuple-element.38.codes), custom_call_target="tpu_custom_call" | custom-call | tf_op jit(solution)/shard_map/early/pallas_call | solution.py:349
  22.3 0.4 %collective-permute-done.first = bf16[80,512]{1,0:T(8,128)(2,1)S(1)} collective-permute-done((bf16[80,512]{1,0:T(8,128)(2,1)S(1)}, bf16[80,512]{1,0:T(8,128)(2,1)S(1)}, u32[]{:S(2)}, u32[]{:S(2)}) %collective-permute-start) | collective-permute-done | bytes 81952 | tf_op jit(solution)/shard_map/ppermute | solution.py:409
  22.6 5.2 %solve.1 = bf16[2,4,64,128]{3,2,1,0:T(8,128)(2,1)} custom-call(bf16[80,512]{1,0:T(8,128)(2,1)S(1)} %collective-permute-done.first, f32[64,64,128]{2,1,0:T(8,128)S(1)} %get-tuple-element.39.partial, f32[64,128]{1,0:T(8,128)S(1)} %get-tuple-element.40.early0, f32[64,128]{1,0:T(8,128)S(1)} %get-tuple-element.41.early1, f32[512,128]{1,0:T(8,128)S(1)} %get-tuple-element.42.pd, ...), custom_call_target="tpu_custom_call" | custom-call | tf_op jit(solution)/shard_map/solve/pallas_call | solution.py:362
Async XLA Ops:
  8.4 11.9 %collective-permute-start.1 = (bf16[80,512]{1,0:T(8,128)(2,1)S(1)}, bf16[80,512]{1,0:T(8,128)(2,1)S(1)}, u32[]{:S(2)}, u32[]{:S(2)}) collective-permute-start(bf16[80,512]{1,0:T(8,128)(2,1)S(1)} %get-tuple-element.33), channel_id=1, source_target_pairs={{0,4},{4,0},{8,12},{12,8},{16,20},{20,16},{24,28},{28,24},{32,36},... | collective-permute-start | bytes 245768 | tf_op jit(solution)/shard_map/ppermute | solution.py:408
  10.0 12.6 %collective-permute-start = (bf16[80,512]{1,0:T(8,128)(2,1)S(1)}, bf16[80,512]{1,0:T(8,128)(2,1)S(1)}, u32[]{:S(2)}, u32[]{:S(2)}) collective-permute-start(bf16[80,512]{1,0:T(8,128)(2,1)S(1)} %get-tuple-element.31), channel_id=1, source_target_pairs={{4,8},{8,4},{12,16},{16,12},{20,24},{24,20},{28,32},{32,28},{36,40... | collective-permute-start | bytes 245768 | tf_op jit(solution)/shard_map/ppermute | solution.py:409

commit v10 on v9

--- a/solution.py
+++ b/solution.py
@@ -137,7 +137,7 @@
     return jnp.where(left, product[0:16], product[16:])
 
 
-def gatherer(sources, codes_of, lows, codes):
+def gatherer(sources, codes_of, lows, codes, hots, fill):
     blocks = 8
     views = dict(zip(codes_of, (ref[:, b * 256 : (b + 1) * 256] for ref, b in sources)))
     zero = jnp.zeros((16, 256), F32)
@@ -154,7 +154,13 @@
     def pick(q, total):
         low = jnp.concatenate([lows[pl.ds(q, 1), :], lows[pl.ds(q + 1, 1), :]], axis=1)
         code = jnp.concatenate([codes[pl.ds(q, 1), :], codes[pl.ds(q + 1, 1), :]], axis=1)
-        found = dot(stacked, jnp.where(counts == low.astype(BF16), high, none))
+        half = pl.multiple_of(q // 2 * 256, 256) if not isinstance(q, int) else q // 2 * 256
+        if fill:
+            hot = jnp.where(counts == low.astype(BF16), high, none)
+            hots[pl.ds(half, 256), :] = hot
+        else:
+            hot = hots[pl.ds(half, 256), :]
+        found = dot(stacked, hot)
         for n, b in enumerate(codes_of):
             part = found[n * HALF : (n + 1) * HALF]
             total = part if total is None else jnp.where(code == b, part, total)
@@ -171,10 +177,10 @@
     return pick
 
 
-def early_kernel(own, second, lows, codes, partial, info0_out, info1_out):
+def early_kernel(own, second, lows, codes, partial, info0_out, info1_out, hots):
     pick = gatherer(
         [(own, b) for b in range(4)] + [(second, b) for b in range(2)],
-        (0, 1, 2, 3, 6, 7), lows, codes,
+        (0, 1, 2, 3, 6, 7), lows, codes, hots, True,
     )
 
     @pl.loop(0, HALF // UE)
@@ -188,7 +194,7 @@
 
 
 def solve_kernel(
-    first, partial, early0, early1, pd, means, weights, lows, codes, out,
+    first, partial, early0, early1, hots, pd, means, weights, lows, codes, out,
     matrix, squares, factors, tails, mixed, shift,
 ):
     lags, spec = out.shape[0], out.shape[1]
@@ -198,7 +204,10 @@
     eye = jnp.where(row == (lanes_of((HALF, 128)) & (HALF - 1)), K - 1.0, 0.0)
     leftb = lanes_of((HALF, 128)) < HALF
     ones = block_diagonal(jnp.ones((HALF, 128), F32), left).astype(BF16)
-    pick = gatherer([(first, b) for b in range(2)], (4, 5), lows, codes)
+    own_half = (lanes_of((128, 128)) < HALF) == (
+        lax.broadcasted_iota(jnp.int32, (128, 128), 0) < HALF
+    )
+    pick = gatherer([(first, b) for b in range(2)], (4, 5), lows, codes, hots, False)
 
     @pl.loop(0, HALF // UA)
     def _(step):
@@ -216,10 +225,11 @@
             pull_high = pull.astype(BF16).astype(F32)
             extra = jnp.concatenate([pull_high, pull - pull_high, jnp.zeros((14, 128), F32)], axis=0)
             lefts.append(jnp.concatenate([weighted, extra.astype(BF16)], axis=0))
-            diagonals.append(block_diagonal(gathered.astype(BF16), leftb))
+            member = gathered.astype(BF16)
+            turned = jnp.concatenate([member, member], axis=0).T
+            diagonals.append(jnp.where(own_half, turned, jnp.zeros_like(turned)))
         products = [
-            lax.dot_general(l, d, (((1,), (1,)), ((), ())), preferred_element_type=F32)
-            for l, d in zip(lefts, diagonals)
+            dot(l, d) for l, d in zip(lefts, diagonals)
         ]
         for q, product in zip(qs, products):
             full = eye + product[0:HALF]
@@ -348,9 +358,10 @@
     shapes = [(HALF, HALF, 128), (HALF, 128), (HALF, 128)]
     return pl.pallas_call(
         early_kernel,
-        out_shape=[jax.ShapeDtypeStruct(x, F32) for x in shapes],
+        out_shape=[jax.ShapeDtypeStruct(x, F32) for x in shapes]
+        + [jax.ShapeDtypeStruct((HALF // 2 * 256, 256), BF16)],
         in_specs=[vmem()] * 4,
-        out_specs=[vmem()] * 3,
+        out_specs=[vmem()] * 4,
         compiler_params=pltpu.CompilerParams(vmem_limit_bytes=SOLVE_BYTES),
         interpret=INTERPRET,
         name="early",
@@ -362,7 +373,7 @@
     return pl.pallas_call(
         solve_kernel,
         out_shape=jax.ShapeDtypeStruct(shape, BF16),
-        in_specs=[vmem()] * 9,
+        in_specs=[vmem()] * 10,
         out_specs=vmem(),
         scratch_shapes=[
             pltpu.VMEM((HALF, HALF, 128), F32),

time: 28 us -> 27 us (0.964)
  Pallas kernels: 9.48 us -> 8.45 us
    pallas_call x1, Pallas kernels: 5.21 us -> 4.13 us  [solve(): pl.pallas_call(solve_kernel, out_shape=jax.ShapeDtypeStruct(shape, BF16),...]
  transfers between devices with their start and end apart: 2 -> 2, of which waited for: 1 -> 1; matrix products, arithmetic and copies ran while one was open for 0% -> 0% of each run, Pallas kernels for 8% -> 9%
where the time goes in v10:
time: 27 us; the launch traced here: 26.8 us
  starting transfers between devices  11.5 us (43%)
  Pallas kernels  8.45 us (31%)
  blocking collectives  5.78 us (21%)
  between operations  0.7 us (3%)
  waiting for transfers between devices  0.32 us (1%)
    ppermute x1, starting transfers between devices, body(): first = lax.ppermute(first, 'space', swaps(tiles, 1))  9.95 us
    all_gather x1, blocking collectives, body(): newest = lax.all_gather(newest, 'lag', axis=0, tiled=True)  5.78 us
    pallas_call x1, Pallas kernels, solve(): pl.pallas_call(solve_kernel, out_shape=jax.ShapeDtypeStruct(shape, BF16),...  4.13 us
    pallas_call x1, Pallas kernels, early(): pl.pallas_call(early_kernel, out_shape=[jax.ShapeDtypeStruct(x, F32) for...  1.97 us
    ppermute x1, starting transfers between devices, body(): second = lax.ppermute(second, 'space', swaps(tiles, 0))  1.58 us
    pallas_call x1, Pallas kernels, observe(): pl.pallas_call(observe_kernel, out_shape=[jax.ShapeDtypeStruct(s, BF16) f...  1.09 us
    pallas_call x1, Pallas kernels, stage(): pl.pallas_call(stage_kernel, out_shape=shapes, in_specs=[anywhere()] * 6,...  0.91 us
  transfers between devices with their start and end apart: 2, of which 1 were waited for; matrix products, arithmetic and copies ran while one was open for 0% of the time, Pallas kernels for 9%

profile of v10, /device:TPU:24, one launch (start us, length us, event | category | flops | bytes accessed | tf_op | source)
XLA Modules:
  0.0 26.8 jit_solution(17122177425348811779)
XLA Ops:
  0.7 0.9 %stage.1 = (bf16[1,4,64,128]{3,2,1,0:T(8,128)(2,1)S(1)}, f32[4,1024]{1,0:T(4,128)S(1)}, s32[1,1024]{1,0:T(1,128)S(1)}, f32[1,1024]{1,0:T(1,128)S(1)}, f32[1,1024]{1,0:T(1,128)S(1)}, /*index=5*/s32[2,512]{1,0:T(2,128)S(1)}) custom-call(bf16[2,4,64,128]{3,2,1,0:T(8,128)(2,1)} %prior.3, f32[4,1024]{1,0:T(4,128)} %coef.1, s32[1,1024]{1,0:T(1,128)} %bitcast.6, ...), custom_call_target="tpu_custom_call" | custom-call | tf_op jit(solution)/shard_map/stage/pallas_call | solution.py:308
  1.6 5.8 %all_gather.3.newest = bf16[4,4,64,128]{3,2,1,0:T(8,128)(2,1)S(1)} all-gather(bf16[1,4,64,128]{3,2,1,0:T(8,128)(2,1)S(1)} %get-tuple-element.26), channel_id=1, replica_groups=mesh['space'=64,'lag'=4] {'lag'}, dimensions={0}, use_global_device_ids=true | all-gather | bytes 327680 | tf_op jit(solution)/shard_map/all_gather | solution.py:415
  7.3 1.1 %observe.1 = (bf16[80,1024]{1,0:T(8,128)(2,1)S(1)}, bf16[80,512]{1,0:T(8,128)(2,1)S(1)}, bf16[80,512]{1,0:T(8,128)(2,1)S(1)}, bf16[2,4,64,128]{3,2,1,0:T(8,128)(...) custom-call(s32[1]{0:T(128)} %bitcast.flag, bf16[4,4,64,128]{3,2,1,0:T(8,128)(2,1)S(1)} %all_gather.3.newest, ...), custom_call_target="tpu_custom_call" | custom-call | tf_op jit(solution)/shard_map/observe/pallas_call | solution.py:324
  8.4 1.6 %collective-permute-start.1 = (bf16[80,512]{1,0:T(8,128)(2,1)S(1)}, bf16[80,512]{1,0:T(8,128)(2,1)S(1)}, u32[]{:S(2)}, u32[]{:S(2)}) collective-permute-start(bf16[80,512]{1,0:T(8,128)(2,1)S(1)} %get-tuple-element.34), channel_id=1, source_target_pairs={{0,4},{4,0},{8,12},{12,8},{16,20},{20,16},{24,28},{28,24},{32,36},... | collective-permute-start | bytes 245768 | tf_op jit(solution)/shard_map/ppermute | solution.py:419
  10.0 10.0 %collective-permute-start = (bf16[80,512]{1,0:T(8,128)(2,1)S(1)}, bf16[80,512]{1,0:T(8,128)(2,1)S(1)}, u32[]{:S(2)}, u32[]{:S(2)}) collective-permute-start(bf16[80,512]{1,0:T(8,128)(2,1)S(1)} %get-tuple-element.32), channel_id=1, source_target_pairs={{4,8},{8,4},{12,16},{16,12},{20,24},{24,20},{28,32},{32,28},{36,40... | collective-permute-start | bytes 245768 | tf_op jit(solution)/shard_map/ppermute | solution.py:420
  20.0 0.4 %prepare.1 = (f32[512,128]{1,0:T(8,128)S(1)}, f32[8,128]{1,0:T(8,128)S(1)}, f32[64,128]{1,0:T(8,128)S(1)}, f32[64,128]{1,0:T(8,128)S(1)}, s32[64,128]{1,0:T(8,128)S(1)}) custom-call(s32[1]{0:T(128)} %bitcast.flag, s32[64,128]{1,0:T(8,128)S(1)} %get-tuple-element.35.index, f32[64,128]{1,0:T(8,128)S(1)} %get-tuple-element.36.local, ...), custom_call_target="tpu_custom_call" | custom-call | tf_op jit(solution)/shard_map/prepare/pallas_call | solution.py:346
  20.4 0.0 collective-permute-done.1.second
  20.4 2.0 %early.1 = (f32[64,64,128]{2,1,0:T(8,128)S(1)}, f32[64,128]{1,0:T(8,128)S(1)}, f32[64,128]{1,0:T(8,128)S(1)}, bf16[8192,256]{1,0:T(8,128)(2,1)S(1)}) custom-call(bf16[80,1024]{1,0:T(8,128)(2,1)S(1)} %get-tuple-element.33.own, bf16[80,512]{1,0:T(8,128)(2,1)S(1)} %collective-permute-done.1.second, f32[64,128]{1,0:T(8,128)S(1)} %get-tuple-element.38.lows, ...), custom_call_target="tpu_custom_call" | custom-call | tf_op jit(solution)/shard_map/early/pallas_call | solution.py:359
  22.3 0.3 %collective-permute-done.first = bf16[80,512]{1,0:T(8,128)(2,1)S(1)} collective-permute-done((bf16[80,512]{1,0:T(8,128)(2,1)S(1)}, bf16[80,512]{1,0:T(8,128)(2,1)S(1)}, u32[]{:S(2)}, u32[]{:S(2)}) %collective-permute-start) | collective-permute-done | bytes 81952 | tf_op jit(solution)/shard_map/ppermute | solution.py:420
  22.6 4.1 %solve.1 = bf16[2,4,64,128]{3,2,1,0:T(8,128)(2,1)} custom-call(bf16[80,512]{1,0:T(8,128)(2,1)S(1)} %collective-permute-done.first, f32[64,64,128]{2,1,0:T(8,128)S(1)} %get-tuple-element.40.partial, f32[64,128]{1,0:T(8,128)S(1)} %get-tuple-element.41.early0, f32[64,128]{1,0:T(8,128)S(1)} %get-tuple-element.42.early1, ...), custom_call_target="tpu_custom_call" | custom-call | tf_op jit(solution)/shard_map/solve/pallas_call | solution.py:373
Async XLA Ops:
  8.4 11.9 %collective-permute-start.1 = (bf16[80,512]{1,0:T(8,128)(2,1)S(1)}, bf16[80,512]{1,0:T(8,128)(2,1)S(1)}, u32[]{:S(2)}, u32[]{:S(2)}) collective-permute-start(bf16[80,512]{1,0:T(8,128)(2,1)S(1)} %get-tuple-element.34), channel_id=1, source_target_pairs={{0,4},{4,0},{8,12},{12,8},{16,20},{20,16},{24,28},{28,24},{32,36},... | collective-permute-start | bytes 245768 | tf_op jit(solution)/shard_map/ppermute | solution.py:419
  10.0 12.6 %collective-permute-start = (bf16[80,512]{1,0:T(8,128)(2,1)S(1)}, bf16[80,512]{1,0:T(8,128)(2,1)S(1)}, u32[]{:S(2)}, u32[]{:S(2)}) collective-permute-start(bf16[80,512]{1,0:T(8,128)(2,1)S(1)} %get-tuple-element.32), channel_id=1, source_target_pairs={{4,8},{8,4},{12,16},{16,12},{20,24},{24,20},{28,32},{32,28},{36,40... | collective-permute-start | bytes 245768 | tf_op jit(solution)/shard_map/ppermute | solution.py:420
